TPU v7x, 512 devices: a whole 4x8x8 slice. The times are simulated.
512 devices in a mesh: freq: 16 (over z_lo, x), tm: 32 (over z_hi, y, core).
Axes of the slice: x: 4, y: 8, z: 8 (z_hi: 2, z_lo: 4; z = z_hi * 4 + z_lo), core: 2. Of those that a mesh axis runs over, the one named last changes fastest.
Arguments:
- baseband: bfloat16 [128, 4, 262144], P('freq', None, 'tm'), may hold values from -3 to 3
- chirp_phase: float32 [128, 16384], P('freq'), may hold values from -3.140625 to 3.140625
- phase_bins: int32 [262144], P('tm'), may hold values from 0 to 1023
Outputs:
- profile: float32 [128, 4, 1024], P('freq', None, 'tm')
Inputs may be any that keep to these rules, and one draw needn't show every extreme that they name: `phase_bins`: each time sample's phase bin.
All inputs are finite; a program needn't handle non-finite values.
Results may differ from a plain program's by a relative error of at most 0.0003.
Values may be sent and summed in bfloat16 or wider, within the bound.
A program may use at most 64 MiB of HBM per device.

v0:
```python
import math

import jax
import jax.numpy as jnp
from jax import lax
from jax.sharding import PartitionSpec as P

BINS = 1024


def shifted(block, axis, distance):
    devices = range(lax.axis_size(axis))
    route = [(i - distance, i) for i in devices if i - distance in devices]
    return lax.ppermute(block, axis, route)


def dft_tables(radix_size):
    indices = jnp.arange(radix_size, dtype=jnp.int32)
    product_small = indices[:, None] * indices[None, :] % radix_size
    angles = product_small.astype(jnp.float32) * (2.0 * math.pi / radix_size)
    product_large = indices[:, None] * indices[None, :] % (radix_size * radix_size)
    twists = product_large.astype(jnp.float32) * (2.0 * math.pi / (radix_size * radix_size))
    return (jnp.cos(angles), -jnp.sin(angles), jnp.cos(twists), -jnp.sin(twists))


def left_product(matrix_real, matrix_imag, vector_real, vector_imag):

    def apply(matrix, vector):
        return jnp.einsum("kn,cpsnm->cpskm", matrix, vector, precision=lax.Precision.HIGH)

    return (
        apply(matrix_real, vector_real) - apply(matrix_imag, vector_imag),
        apply(matrix_real, vector_imag) + apply(matrix_imag, vector_real),
    )


def right_product(vector_real, vector_imag, matrix_real, matrix_imag):

    def apply(vector, matrix):
        return jnp.einsum("cpskn,nm->cpskm", vector, matrix, precision=lax.Precision.HIGH)

    return (
        apply(vector_real, matrix_real) - apply(vector_imag, matrix_imag),
        apply(vector_real, matrix_imag) + apply(vector_imag, matrix_real),
    )


def filter_frames(frames, response_real, response_imag, tables):
    four_real, four_imag, twist_real, twist_imag = tables
    channels, _, frame_count, frame_len = frames.shape
    radix_size = four_real.shape[0]
    keep_count = frame_len // 2
    shaped = frames.reshape(channels, 2, 2, frame_count, radix_size, radix_size)
    input_real = shaped[:, :, 0]
    input_imag = shaped[:, :, 1]
    section_real, section_imag = left_product(four_real, four_imag, input_real, input_imag)
    turned_real = section_real * twist_real - section_imag * twist_imag
    turned_imag = section_real * twist_imag + section_imag * twist_real
    spec_real, spec_imag = right_product(turned_real, turned_imag, four_real, four_imag)
    gain_real = response_real[:, None, None]
    gain_imag = response_imag[:, None, None]
    shaped_real = spec_real * gain_real - spec_imag * gain_imag
    shaped_imag = spec_real * gain_imag + spec_imag * gain_real
    back_real, back_imag = right_product(shaped_real, shaped_imag, four_real, -four_imag)
    untwist_real = back_real * twist_real + back_imag * twist_imag
    untwist_imag = back_imag * twist_real - back_real * twist_imag
    wave_real, wave_imag = left_product(four_real, -four_imag, untwist_real, untwist_imag)
    factor = 1.0 / frame_len
    wave_real = wave_real.reshape(channels, 2, frame_count, frame_len)[..., keep_count:] * factor
    wave_imag = wave_imag.reshape(channels, 2, frame_count, frame_len)[..., keep_count:] * factor
    return (wave_real, wave_imag)


def fold_blocks(stokes, phase_bins):
    channels, _, samples = stokes.shape
    width = min(1024, samples)
    count = samples // width
    bin_ids = jnp.arange(BINS, dtype=jnp.int32)

    def add_block(index, total):
        start = index * width
        part_bins = lax.dynamic_slice_in_dim(phase_bins, start, width, 0)
        part_stokes = lax.dynamic_slice_in_dim(stokes, start, width, 2)
        onehot = (part_bins[:, None] == bin_ids[None, :]).astype(jnp.float32)
        return total + jnp.einsum("cjt,tb->cjb", part_stokes, onehot, precision=lax.Precision.HIGH)

    return lax.fori_loop(0, count, add_block, jnp.zeros((channels, 4, BINS), jnp.float32))


def shards(baseband, chirp_phase, phase_bins):
    channels, _, samples = baseband.shape
    frame_len = chirp_phase.shape[1]
    keep_count = frame_len // 2
    radix_size = math.isqrt(frame_len)
    segments = samples // keep_count
    tables = dft_tables(radix_size)
    turned = chirp_phase.reshape(channels, radix_size, radix_size).transpose(0, 2, 1)
    response_real = jnp.cos(turned)
    response_imag = jnp.sin(turned)
    rim_samples = shifted(baseband, "tm", 1)
    extended = jnp.concatenate([rim_samples, baseband], axis=2).astype(jnp.float32)
    blocks = extended.reshape(channels, 4, segments + 1, keep_count)
    frames = jnp.concatenate([blocks[:, :, :-1], blocks[:, :, 1:]], axis=3)
    wave_real, wave_imag = filter_frames(frames, response_real, response_imag, tables)
    first_real = wave_real[:, 0].reshape(channels, samples)
    first_imag = wave_imag[:, 0].reshape(channels, samples)
    second_real = wave_real[:, 1].reshape(channels, samples)
    second_imag = wave_imag[:, 1].reshape(channels, samples)
    power_first = first_real * first_real + first_imag * first_imag
    power_second = second_real * second_real + second_imag * second_imag
    stokes = jnp.stack(
        [
            power_first + power_second,
            power_first - power_second,
            2.0 * (first_real * second_real + first_imag * second_imag),
            2.0 * (first_real * second_imag - first_imag * second_real),
        ],
        axis=1,
    )
    folded = fold_blocks(stokes, phase_bins)
    factor = 1.0 / float(samples * lax.axis_size("tm") // BINS)
    summed = lax.psum(folded, "tm")
    part_width = BINS // lax.axis_size("tm")
    profile_part = lax.dynamic_slice_in_dim(
        summed, lax.axis_index("tm") * part_width, part_width, 2
    )
    return profile_part * factor


def solution(mesh):
    placed = (P("freq", None, "tm"), P("freq", None), P("tm"))
    return jax.shard_map(
        shards, mesh=mesh, in_specs=placed, out_specs=P("freq", None, "tm"), check_vma=False
    )
```

profile of v0, /device:TPU:1, one launch (start us, length us, event | category | flops | bytes accessed | tf_op | source)
XLA Modules:
  0.0 407.9 jit_solution(17535864532734620487)
XLA Ops:
  6.5 4.7 %collective-permute-start = (bf16[8,4,8192]{2,1,0:T(4,128)(2,1)}, bf16[8,4,8192]{2,1,0:T(4,128)(2,1)S(1)}, u32[]{:S(2)}, u32[]{:S(2)}) collective-permute-start(bf16[8,4,8192]{2,1,0:T(4,128)(2,1)} %param.5), channel_id=1, source_target_pairs={{0,1},{1,2},{2,3},{3,4},{4,5},{5,6},{6,7},{7,8},{8,9},{9,10},{10,1... | collective-permute-start | bytes 1572872 | tf_op jit(solution)/shard_map/ppermute | solution.py:14
  11.7 2.8 cosine_bitcast_fusion
  15.0 2.7 collective-permute-done
  18.5 1.8 pad_maximum_fusion
  20.3 2.9 reshape.302
  23.2 1.1 fusion.21
  24.3 1.1 fusion.22
  25.4 1.1 fusion.14
  26.6 1.1 fusion.13
  27.7 1.2 fusion.19
  28.9 1.2 fusion.17
  30.1 1.2 convolution_subtract_fusion.2
  31.4 1.2 convolution_add_fusion.2
  34.5 1.1 convolution_add_fusion.1
  36.6 1.2 fusion.23
  37.7 1.2 fusion.24
  38.9 2.2 fusion.12
  41.1 2.6 copy.56
  44.8 1.1 copy_multiply_fusion.1
  45.9 2.2 fusion.11
  48.1 1.6 copy.60
  50.3 16.3 %while.14 = (s32[]{:T(128)}, f32[8,4,1024]{2,0,1:T(8,128)S(1)}, f32[8,4,8192]{2,0,1:T(8,128)S(1)}, s32[8192]{0:T(1024)}, s32[]{:T(128)}, /*index=5*/s32[]{:T(128)}, s32[]{:T(128)}, s32[]{:T(128)}) while((s32[]{:T(128)}, f32[8,4,1024]{2,0,1:T(8,128)S(1)}, f32[8,4,8192]{2,0,1:T(8,128)S(1)}, s32[8192]{0:T(1024)}, s32[]{:T(128)}, ...), condition=%wide.region_1.2_spmd.clone, body=%wide.region_0.1_spmd.clone.sunk | while | flops 202440704 | bytes 405653 | solution.py:87
  51.0 1.3 fusion.147
  53.1 1.3 fusion.147
  55.1 1.3 fusion.147
  57.1 1.3 fusion.147
  59.2 1.3 fusion.147
  61.2 1.3 fusion.147
  63.2 1.3 fusion.147
  65.3 1.3 fusion.147
  67.4 332.3 %all-reduce.2.cloned.1.call-done = f32[8,4,1024]{2,1,0:T(4,128)} async-done(((f32[8,4,1024]{2,1,0:T(4,128)}), f32[8,4,1024]{2,1,0:T(4,128)}) %all-reduce.2.cloned.1.call-update) | async-done | bytes 131088 | tf_op jit(solution)/shard_map/psum | solution.py:122
  399.7 1.4 dynamic-slice_multiply_fusion
  (31 shorter events, 12.5 us)
Async XLA Ops:
  6.5 11.1 %copy-start.1 = (bf16[8,4,8192]{2,1,0:T(4,128)(2,1)S(1)}, bf16[8,4,8192]{2,1,0:T(4,128)(2,1)}, u32[]{:S(2)}) copy-start(bf16[8,4,8192]{2,1,0:T(4,128)(2,1)} %param.5) | copy-start | bytes 1572868
  6.5 393.1 %all-reduce.2.cloned.1.call-start = ((), (), s32[]{:S(2)}) async-start(), calls=%async_computation | async-start | bytes 262144 | tf_op jit(solution)/shard_map/psum | solution.py:122
  6.5 11.1 %collective-permute-start = (bf16[8,4,8192]{2,1,0:T(4,128)(2,1)}, bf16[8,4,8192]{2,1,0:T(4,128)(2,1)S(1)}, u32[]{:S(2)}, u32[]{:S(2)}) collective-permute-start(bf16[8,4,8192]{2,1,0:T(4,128)(2,1)} %param.5), channel_id=1, source_target_pairs={{0,1},{1,2},{2,3},{3,4},{4,5},{5,6},{6,7},{7,8},{8,9},{9,10},{10,1... | collective-permute-start | bytes 1572872 | tf_op jit(solution)/shard_map/ppermute | solution.py:14
  48.1 2.0 copy-start
Sparse Core Ops, SparseCore 0:
  67.5 332.1 all-reduce.1
where the time goes:
time: 408 us
  waiting for transfers between devices  335 us (82%)
  matrix products  30.5 us (7%)
  local copies, waits for them, and re-layouts  18.1 us (4%)
  between operations  13.6 us (3%)
  other arithmetic  5.86 us (1%)
  starting transfers between devices  4.7 us (1%)
    psum x1, waiting for transfers between devices, shards(): summed = lax.psum(folded, 'tm')  332 us
    dot_general x8, matrix products, apply(): jnp.einsum('kn,cpsnm->cpskm', matrix, vector, precision=lax.Precision.HIGH)  11.1 us
    dot_general x8, matrix products, add_block(): jnp.einsum('cjt,tb->cjb', part_stokes, onehot, precision=lax.Precision.HIGH)  10.5 us
    dot_general x8, matrix products, apply(): jnp.einsum('cpskn,nm->cpskm', vector, matrix, precision=lax.Precision.HIGH)  8.81 us
  transfers between devices with their start and end apart: 2, of which 2 were waited for; matrix products, arithmetic and copies ran while one was open for 1% of the time, Pallas kernels for 0%

commit v1 on v0

v1 whole, which is shorter than its diff:
```python
import functools

import jax
import jax.numpy as jnp
import numpy as np
from jax import lax
from jax.experimental import pallas as pl
from jax.experimental.pallas import tpu as pltpu
from jax.sharding import PartitionSpec as P

BINS = 1024
RADIX = 128
HALF = 64
LOW_BINS = 256
F32 = jnp.float32
BF16 = jnp.bfloat16


def split_table(table):
    high = table.astype(jnp.bfloat16)
    low = (table - high.astype(np.float64)).astype(jnp.bfloat16)
    return high, low


def dft_tables():
    index = np.arange(RADIX)
    angle = 2.0 * np.pi * (index[:, None] * index[None, :] % RADIX) / RADIX
    four_real, four_imag = np.cos(angle), -np.sin(angle)
    turn = 2.0 * np.pi * (index[:, None] * index[None, :]) / (RADIX * RADIX)
    twist = np.concatenate([np.cos(turn), -np.sin(turn)], axis=1).astype(np.float32)
    left = np.block([[four_real, -four_imag], [four_imag, four_real]])
    right = np.block([[four_real, four_imag], [-four_imag, four_real]])
    back_right = np.block([[four_real, -four_imag], [four_imag, four_real]]) / RADIX
    kept_real, kept_imag = four_real[HALF:], four_imag[HALF:]
    back_left = np.block([[kept_real, kept_imag], [-kept_imag, kept_real]]) / RADIX
    tables = []
    for table in (left, right, back_right, back_left):
        tables.extend(split_table(table))
    return tables, twist


def halves(value):
    high = value.astype(BF16)
    low = (value - high.astype(F32)).astype(BF16)
    return high, low


def dot(a, b):
    return jnp.dot(a, b, preferred_element_type=F32)


def cos_sin(phase):
    half = phase * 0.5
    square = half * half
    sine = half * (
        1.0 + square * (-1.0 / 6 + square * (1.0 / 120 + square * (-1.0 / 5040 + square * (
            1.0 / 362880 + square * (-1.0 / 39916800 + square * (1.0 / 6227020800))))))
    )
    cosine = 1.0 + square * (-1.0 / 2 + square * (1.0 / 24 + square * (-1.0 / 720 + square * (
        1.0 / 40320 + square * (-1.0 / 3628800 + square * (
            1.0 / 479001600 + square * (-1.0 / 87178291200))))))
    )
    return 1.0 - 2.0 * sine * sine, 2.0 * sine * cosine


def work_kernel(
    channels, prev, cur, chirp, bins, left_h, left_l, right_h, right_l, back_right_h,
    back_right_l, back_left_h, back_left_l, twist, out, stokes, picked, onehot,
):
    rows = 4 * channels
    twist_real = twist[:, :RADIX]
    twist_imag = twist[:, RADIX:]
    wide_real = jnp.concatenate([twist_real, twist_real], axis=1)
    wide_imag = jnp.concatenate([twist_imag, twist_imag], axis=1)

    def channel(c, carry):
        base = 4 * c

        def pair(part):
            old = jnp.concatenate([prev[base + part], prev[base + 2 + part]], axis=1)
            new = jnp.concatenate([cur[base + part], cur[base + 2 + part]], axis=1)
            return jnp.concatenate([old, new], axis=0)

        series = jnp.concatenate([pair(0), pair(1)], axis=0)
        section = dot(left_h[...], series) + dot(left_l[...], series)
        real, imag = section[:RADIX], section[RADIX:]
        turned_real = real * wide_real - imag * wide_imag
        turned_imag = real * wide_imag + imag * wide_real
        gain_real, gain_imag = cos_sin(chirp[c].T)
        waves_real, waves_imag = [], []
        for p in range(2):
            lanes = slice(p * RADIX, (p + 1) * RADIX)
            high, low = halves(
                jnp.concatenate([turned_real[:, lanes], turned_imag[:, lanes]], axis=1)
            )
            spec = dot(high, right_h[...]) + dot(low, right_h[...]) + dot(high, right_l[...])
            spec_real, spec_imag = spec[:, :RADIX], spec[:, RADIX:]
            high, low = halves(
                jnp.concatenate(
                    [
                        spec_real * gain_real - spec_imag * gain_imag,
                        spec_real * gain_imag + spec_imag * gain_real,
                    ],
                    axis=1,
                )
            )
            back = (
                dot(high, back_right_h[...])
                + dot(low, back_right_h[...])
                + dot(high, back_right_l[...])
            )
            back_real, back_imag = back[:, :RADIX], back[:, RADIX:]
            waves_real.append(back_real * twist_real + back_imag * twist_imag)
            waves_imag.append(back_imag * twist_real - back_real * twist_imag)
        high, low = halves(
            jnp.concatenate(
                [jnp.concatenate(waves_real, axis=1), jnp.concatenate(waves_imag, axis=1)], axis=0
            )
        )
        wave = (
            dot(back_left_h[...], high) + dot(back_left_h[...], low) + dot(back_left_l[...], high)
        )
        xr, xi = wave[:HALF, :RADIX], wave[HALF:, :RADIX]
        yr, yi = wave[:HALF, RADIX:], wave[HALF:, RADIX:]
        first = xr * xr + xi * xi
        second = yr * yr + yi * yi
        stokes[pl.ds(base, HALF, rows), :] = first + second
        stokes[pl.ds(base + 1, HALF, rows), :] = first - second
        stokes[pl.ds(base + 2, HALF, rows), :] = 2.0 * (xr * yr + xi * yi)
        stokes[pl.ds(base + 3, HALF, rows), :] = 2.0 * (xr * yi - xi * yr)
        return carry

    lax.fori_loop(0, channels, channel, 0)

    groups = BINS // LOW_BINS
    lane_bins = lax.broadcasted_iota(jnp.int32, (LOW_BINS, 2 * RADIX), 0)

    def pick(m, carry):
        start = pl.multiple_of(m * 2 * rows, 2 * rows)
        value = jnp.concatenate(
            [stokes[pl.ds(start, rows), :], stokes[pl.ds(start + rows, rows), :]], axis=1
        )
        high = value.astype(BF16).astype(F32)
        both = jnp.concatenate([high, value - high], axis=0)
        own = bins[pl.ds(m, 1), :]
        group = own // LOW_BINS
        columns = pl.ds(pl.multiple_of(m * 2 * RADIX, 2 * RADIX), 2 * RADIX)
        for q in range(groups):
            picked[pl.ds(q * 2 * rows, 2 * rows), columns] = jnp.where(
                group == q, both, 0.0
            ).astype(BF16)
        onehot[:, columns] = jnp.where(
            lane_bins == own - group * LOW_BINS, 1.0, 0.0
        ).astype(BF16)
        return carry

    lax.fori_loop(0, HALF // 2, pick, 0)

    total = lax.dot_general(
        picked[...], onehot[...], (((1,), (1,)), ((), ())), preferred_element_type=F32
    )
    for q in range(groups):
        at = q * 2 * rows
        folded = total[at:at + rows] + total[at + rows:at + 2 * rows]
        for h in range(2):
            for b in range(4):
                lanes = slice(h * RADIX + 32 * b, h * RADIX + 32 * b + 32)
                out[q * 8 + h * 4 + b] = jnp.concatenate(
                    [folded[8 * a:8 * a + 8, lanes] for a in range(4)], axis=1
                )


def sum_kernel(devices, factor, tiles, out, landed, send_sems, recv_sems):
    me = lax.axis_index("tm")

    barrier = pltpu.get_barrier_semaphore()

    def greet(i, carry):
        pl.semaphore_signal(
            barrier, inc=1, device_id={"tm": lax.rem(me + i, devices)},
            device_id_type=pl.DeviceIdType.MESH,
        )
        return carry

    lax.fori_loop(1, devices, greet, 0)
    pl.semaphore_wait(barrier, devices - 1)

    def copy(i):
        peer = lax.rem(me + i, devices)
        return pltpu.make_async_remote_copy(
            src_ref=tiles.at[peer],
            dst_ref=landed.at[i],
            send_sem=send_sems.at[i],
            recv_sem=recv_sems.at[i],
            device_id={"tm": peer},
            device_id_type=pl.DeviceIdType.MESH,
        )

    def send(i, carry):
        copy(i).start()
        return carry

    lax.fori_loop(1, devices, send, 0)

    def take(i, total):
        copy(i).wait_recv()
        return total + landed[i]

    total = lax.fori_loop(1, devices, take, tiles[me]) * factor
    for a in range(4):
        for k in range(2):
            out[2 * a + k] = total[4 * k:4 * k + 4, 32 * a:32 * a + 32]

    def drain(i, carry):
        copy(i).wait_send()
        return carry

    lax.fori_loop(1, devices, drain, 0)


def shards(baseband, chirp_phase, phase_bins):
    channels, _, samples = baseband.shape
    devices = lax.axis_size("tm")
    rows = 4 * channels
    cur = baseband.reshape(rows, HALF, RADIX)
    prev = lax.ppermute(cur, "tm", [(i, i + 1) for i in range(devices - 1)])
    chirp = chirp_phase.reshape(channels, RADIX, RADIX)
    bins = phase_bins.reshape(samples // (2 * RADIX), 2 * RADIX)
    tables, twist = dft_tables()
    in_vmem = pl.BlockSpec(memory_space=pltpu.VMEM)
    tiles = pl.pallas_call(
        functools.partial(work_kernel, channels),
        out_shape=jax.ShapeDtypeStruct((devices, 8, RADIX), F32),
        in_specs=[in_vmem] * 13,
        out_specs=in_vmem,
        scratch_shapes=[
            pltpu.VMEM((HALF * rows, RADIX), F32),
            pltpu.VMEM((8 * rows, samples), BF16),
            pltpu.VMEM((LOW_BINS, samples), BF16),
        ],
        name="work",
    )(prev, cur, chirp, bins, *tables, twist)
    factor = 1.0 / float(samples * devices // BINS)
    return pl.pallas_call(
        functools.partial(sum_kernel, devices, factor),
        out_shape=jax.ShapeDtypeStruct((channels, 4, BINS // devices), F32),
        in_specs=[in_vmem],
        out_specs=in_vmem,
        scratch_shapes=[
            pltpu.VMEM((devices, 8, RADIX), F32),
            pltpu.SemaphoreType.DMA((devices,)),
            pltpu.SemaphoreType.DMA((devices,)),
        ],
        compiler_params=pltpu.CompilerParams(collective_id=0, has_side_effects=True),
        name="sum",
    )(tiles)


def solution(mesh):
    placed = (P("freq", None, "tm"), P("freq", None), P("tm"))
    return jax.shard_map(
        shards, mesh=mesh, in_specs=placed, out_specs=P("freq", None, "tm"), check_vma=False
    )
```

time: 408 us -> 62.6 us (0.15)
  waiting for transfers between devices: 335 us -> 4.56 us
  Pallas kernels: 0 us -> 47.8 us
  matrix products: 30.5 us -> 0 us
  between operations: 13.6 us -> 0.04 us
  local copies, waits for them, and re-layouts: 18.1 us -> 5.3 us
  other arithmetic: 5.86 us -> 0 us
    psum x1 -> x0, waiting for transfers between devices: 332 us -> none  [shards(): summed = lax.psum(folded, 'tm')]
    pallas_call x0 -> x2, Pallas kernels: none -> 47.8 us  [the longest x1 33.5 us: shards(): pl.pallas_call(functools.partial(sum_kernel, devices, factor), out_shape=...]
    dot_general x24 -> x0, matrix products: 30.5 us -> none  [the longest x8 11.1 us: apply(): jnp.einsum('kn,cpsnm->cpskm', matrix, vector, precision=lax.Precision.HIGH)]
    dynamic_slice x8 -> x0, local copies, waits for them, and re-layouts: 5.54 us -> none  [add_block(): part_bins = lax.dynamic_slice_in_dim(phase_bins, start, width, 0)]
  transfers between devices with their start and end apart: 2 -> 1, of which waited for: 2 -> 1; matrix products, arithmetic and copies ran while one was open for 1% -> 2% of each run, Pallas kernels for 0% -> 0%
where the time goes in v1:
time: 62.6 us; the launch traced here: 62.3 us
  Pallas kernels  47.8 us (76%)
  local copies, waits for them, and re-layouts  5.3 us (8%)
  starting transfers between devices  4.58 us (7%)
  waiting for transfers between devices  4.56 us (7%)
    pallas_call x1, Pallas kernels, shards(): pl.pallas_call(functools.partial(sum_kernel, devices, factor), out_shape=...  33.5 us
    pallas_call x1, Pallas kernels, shards(): pl.pallas_call(functools.partial(work_kernel, channels), out_shape=jax.Sh...  14.3 us
    ppermute x1, starting transfers between devices, shards(): prev = lax.ppermute(cur, 'tm', [(i, i + 1) for i in range(devices - 1)])  4.58 us
    ppermute x1, waiting for transfers between devices, shards(): prev = lax.ppermute(cur, 'tm', [(i, i + 1) for i in range(devices - 1)])  4.56 us
    unnamed x10, local copies, waits for them, and re-layouts  3.04 us
    reshape x1, local copies, waits for them, and re-layouts, shards(): cur = baseband.reshape(rows, HALF, RADIX)  1.64 us
  transfers between devices with their start and end apart: 1, of which 1 were waited for; matrix products, arithmetic and copies ran while one was open for 2% of the time, Pallas kernels for 0%

profile of v1, /device:TPU:1, one launch (start us, length us, event | category | flops | bytes accessed | tf_op | source)
XLA Modules:
  0.0 62.3 jit_solution(3916031353620622837)
XLA Ops:
  0.0 0.0 copy-start.3
  0.0 0.0 copy-start.1
  0.0 1.6 %reshape.9.cur = bf16[32,64,128]{2,1,0:T(8,128)(2,1)S(1)} reshape(bf16[8,4,8192]{2,1,0:T(4,128)(2,1)} %param.12) | data formatting | bytes 1048576 | tf_op jit(solution)/shard_map/reshape | solution.py:225
  1.6 0.0 copy-start
  1.7 4.6 %collective-permute-start = (bf16[32,64,128]{2,1,0:T(8,128)(2,1)S(1)}, bf16[32,64,128]{2,1,0:T(8,128)(2,1)S(1)}, u32[]{:S(2)}, u32[]{:S(2)}) collective-permute-start(bf16[32,64,128]{2,1,0:T(8,128)(2,1)S(1)} %reshape.9.cur), channel_id=1, source_target_pairs={{0,1},{1,2},{2,3},{3,4},{4,5},{5,6},{6,7},{7,8},{8,9},{9,10},{10,1... | collective-permute-start | bytes 1572872 | tf_op jit(solution)/shard_map/ppermute | solution.py:226
  6.2 0.0 copy-done.3
  6.3 0.6 %reshape.11.bins = s32[32,256]{1,0:T(8,128)} reshape(s32[8192]{0:T(1024)S(1)} %copy-done.3) | data formatting | bytes 65536 | tf_op jit(solution)/shard_map/reshape | solution.py:228
  6.9 0.0 copy-done.1
  6.9 0.9 %copy.15 = f32[1,8,128,128]{3,2,1,0:T(8,128)} copy(f32[1,8,128,128]{3,1,2,0:T(8,128)S(1)} %bitcast.5) | data formatting | bytes 1048576
  7.8 0.0 copy-done
  7.8 4.6 %collective-permute-done.prev = bf16[32,64,128]{2,1,0:T(8,128)(2,1)S(1)} collective-permute-done((bf16[32,64,128]{2,1,0:T(8,128)(2,1)S(1)}, bf16[32,64,128]{2,1,0:T(8,128)(2,1)S(1)}, u32[]{:S(2)}, u32[]{:S(2)}) %collective-permute-start) | collective-permute-done | bytes 524320 | tf_op jit(solution)/shard_map/ppermute | solution.py:226
  12.4 0.0 copy-start.2
  12.4 0.8 %copy-done.2 = bf16[32,64,128]{2,1,0:T(8,128)(2,1)} copy-done((bf16[32,64,128]{2,1,0:T(8,128)(2,1)}, bf16[32,64,128]{2,1,0:T(8,128)(2,1)S(1)}, u32[]{:S(2)}) %copy-start.2) | copy-done | bytes 524312
  13.2 14.3 %work.1.tiles = f32[32,8,128]{2,1,0:T(8,128)} custom-call(bf16[32,64,128]{2,1,0:T(8,128)(2,1)} %copy-done.2, bf16[32,64,128]{2,1,0:T(8,128)(2,1)} %copy-done, f32[8,128,128]{2,1,0:T(8,128)} %bitcast.4, s32[32,256]{1,0:T(8,128)} %reshape.11.bins, bf16[256,256]{1,0:T(8,128)(2,1)} %constant.18.clone.left_h, bf16[256,256]{1,0:T(8,128)(2,1)} %constant.19.clone.left_l, ...), custom_call_target="tpu_custom_call" | custom-call | tf_op jit(solution)/shard_map/work/pallas_call | solution.py:231
  27.5 33.5 %sum.1 = f32[8,4,32]{2,1,0:T(4,128)} custom-call(f32[32,8,128]{2,1,0:T(8,128)} %work.1.tiles), custom_call_target="tpu_custom_call" | custom-call | tf_op jit(solution)/shard_map/sum/pallas_call | solution.py:244
  61.0 1.3 %copy.17 = f32[8,4,32]{2,1,0:T(4,128)} copy(f32[8,4,32]{2,1,0:T(4,128)} %sum.1) | data formatting | bytes 8192
Async XLA Ops:
  0.0 6.2 %copy-start.3 = (s32[8192]{0:T(1024)S(1)}, s32[8192]{0:T(1024)}, u32[]{:S(2)}) copy-start(s32[8192]{0:T(1024)} %param.14) | copy-start | bytes 98308
  0.0 6.9 %copy-start.1 = (f32[8,16384]{1,0:T(8,128)S(1)}, f32[8,16384]{1,0:T(8,128)}, u32[]{:S(2)}) copy-start(f32[8,16384]{1,0:T(8,128)} %param.13) | copy-start | bytes 1572868
  1.6 6.1 %copy-start = (bf16[32,64,128]{2,1,0:T(8,128)(2,1)}, bf16[32,64,128]{2,1,0:T(8,128)(2,1)S(1)}, u32[]{:S(2)}) copy-start(bf16[32,64,128]{2,1,0:T(8,128)(2,1)S(1)} %reshape.9.cur) | copy-start | bytes 1572868
  1.7 10.7 %collective-permute-start = (bf16[32,64,128]{2,1,0:T(8,128)(2,1)S(1)}, bf16[32,64,128]{2,1,0:T(8,128)(2,1)S(1)}, u32[]{:S(2)}, u32[]{:S(2)}) collective-permute-start(bf16[32,64,128]{2,1,0:T(8,128)(2,1)S(1)} %reshape.9.cur), channel_id=1, source_target_pairs={{0,1},{1,2},{2,3},{3,4},{4,5},{5,6},{6,7},{7,8},{8,9},{9,10},{10,1... | collective-permute-start | bytes 1572872 | tf_op jit(solution)/shard_map/ppermute | solution.py:226
  12.4 0.8 %copy-start.2 = (bf16[32,64,128]{2,1,0:T(8,128)(2,1)}, bf16[32,64,128]{2,1,0:T(8,128)(2,1)S(1)}, u32[]{:S(2)}) copy-start(bf16[32,64,128]{2,1,0:T(8,128)(2,1)S(1)} %collective-permute-done.prev) | copy-start | bytes 1572868

commit v2 on v1

--- a/solution.py
+++ b/solution.py
@@ -34,7 +34,10 @@
     kept_real, kept_imag = four_real[HALF:], four_imag[HALF:]
     back_left = np.block([[kept_real, kept_imag], [-kept_imag, kept_real]]) / RADIX
     tables = []
-    for table in (left, right, back_right, back_left):
+    for part in range(2):
+        columns = np.arange(4 * HALF).reshape(4, HALF)[part::2].reshape(-1)
+        tables.append(np.concatenate(split_table(left[:, columns]), axis=1))
+    for table in (right, back_right, back_left):
         tables.extend(split_table(table))
     return tables, twist
 
@@ -63,30 +66,67 @@
     return 1.0 - 2.0 * sine * sine, 2.0 * sine * cosine
 
 
+def paired(block, base, part):
+    return jnp.concatenate([block[base + part], block[base + 2 + part]], axis=1)
+
+
+def first_stage(table, block, base):
+    series = jnp.concatenate([paired(block, base, 0), paired(block, base, 1)], axis=0)
+    return dot(table[...], jnp.concatenate([series, series], axis=0))
+
+
+def prep_kernel(channels, cur, chirp, bins, left, gain, part, onehot):
+    lane_bins = lax.broadcasted_iota(jnp.int32, (LOW_BINS, 2 * RADIX), 0)
+
+    def channel(c, carry):
+        cosine, sine = cos_sin(chirp[c].T)
+        gain[c] = jnp.concatenate([cosine, sine], axis=1)
+        part[c] = first_stage(left, cur, 4 * c)
+        return carry
+
+    lax.fori_loop(0, channels, channel, 0)
+
+    def mark(m, carry):
+        own = bins[pl.ds(m, 1), :]
+        columns = pl.ds(pl.multiple_of(m * 2 * RADIX, 2 * RADIX), 2 * RADIX)
+        onehot[:, columns] = jnp.where(
+            lane_bins == own - own // LOW_BINS * LOW_BINS, 1.0, 0.0
+        ).astype(BF16)
+        return carry
+
+    lax.fori_loop(0, HALF // 2, mark, 0)
+
+
 def work_kernel(
-    channels, prev, cur, chirp, bins, left_h, left_l, right_h, right_l, back_right_h,
-    back_right_l, back_left_h, back_left_l, twist, out, stokes, picked, onehot,
+    channels, devices, factor, prev, gain, part, onehot, bins, left, right_h, right_l,
+    back_right_h, back_right_l, back_left_h, back_left_l, twist, out, stokes, picked, tiles,
+    landed, send_sems, recv_sems,
 ):
+    me = lax.axis_index("tm")
+    barrier = pltpu.get_barrier_semaphore()
+
+    def greet(i, carry):
+        pl.semaphore_signal(
+            barrier, inc=1, device_id={"tm": lax.rem(me + i, devices)},
+            device_id_type=pl.DeviceIdType.MESH,
+        )
+        return carry
+
+    lax.fori_loop(1, devices, greet, 0)
+
     rows = 4 * channels
     twist_real = twist[:, :RADIX]
     twist_imag = twist[:, RADIX:]
     wide_real = jnp.concatenate([twist_real, twist_real], axis=1)
     wide_imag = jnp.concatenate([twist_imag, twist_imag], axis=1)
 
-    def channel(c, carry):
+    def channel(c):
         base = 4 * c
-
-        def pair(part):
-            old = jnp.concatenate([prev[base + part], prev[base + 2 + part]], axis=1)
-            new = jnp.concatenate([cur[base + part], cur[base + 2 + part]], axis=1)
-            return jnp.concatenate([old, new], axis=0)
-
-        series = jnp.concatenate([pair(0), pair(1)], axis=0)
-        section = dot(left_h[...], series) + dot(left_l[...], series)
+        section = part[c] + first_stage(left, prev, base)
         real, imag = section[:RADIX], section[RADIX:]
         turned_real = real * wide_real - imag * wide_imag
         turned_imag = real * wide_imag + imag * wide_real
-        gain_real, gain_imag = cos_sin(chirp[c].T)
+        gain_real, gain_imag = gain[c, :, :RADIX], gain[c, :, RADIX:]
         waves_real, waves_imag = [], []
         for p in range(2):
             lanes = slice(p * RADIX, (p + 1) * RADIX)
@@ -128,12 +168,15 @@
         stokes[pl.ds(base + 1, HALF, rows), :] = first - second
         stokes[pl.ds(base + 2, HALF, rows), :] = 2.0 * (xr * yr + xi * yi)
         stokes[pl.ds(base + 3, HALF, rows), :] = 2.0 * (xr * yi - xi * yr)
-        return carry
-
-    lax.fori_loop(0, channels, channel, 0)
+
+    def channel_pair(i, carry):
+        channel(2 * i)
+        channel(2 * i + 1)
+        return carry
+
+    lax.fori_loop(0, channels // 2, channel_pair, 0)
 
     groups = BINS // LOW_BINS
-    lane_bins = lax.broadcasted_iota(jnp.int32, (LOW_BINS, 2 * RADIX), 0)
 
     def pick(m, carry):
         start = pl.multiple_of(m * 2 * rows, 2 * rows)
@@ -142,16 +185,12 @@
         )
         high = value.astype(BF16).astype(F32)
         both = jnp.concatenate([high, value - high], axis=0)
-        own = bins[pl.ds(m, 1), :]
-        group = own // LOW_BINS
+        group = bins[pl.ds(m, 1), :] // LOW_BINS
         columns = pl.ds(pl.multiple_of(m * 2 * RADIX, 2 * RADIX), 2 * RADIX)
         for q in range(groups):
             picked[pl.ds(q * 2 * rows, 2 * rows), columns] = jnp.where(
                 group == q, both, 0.0
             ).astype(BF16)
-        onehot[:, columns] = jnp.where(
-            lane_bins == own - group * LOW_BINS, 1.0, 0.0
-        ).astype(BF16)
         return carry
 
     lax.fori_loop(0, HALF // 2, pick, 0)
@@ -165,24 +204,10 @@
         for h in range(2):
             for b in range(4):
                 lanes = slice(h * RADIX + 32 * b, h * RADIX + 32 * b + 32)
-                out[q * 8 + h * 4 + b] = jnp.concatenate(
+                tiles[q * 8 + h * 4 + b] = jnp.concatenate(
                     [folded[8 * a:8 * a + 8, lanes] for a in range(4)], axis=1
                 )
 
-
-def sum_kernel(devices, factor, tiles, out, landed, send_sems, recv_sems):
-    me = lax.axis_index("tm")
-
-    barrier = pltpu.get_barrier_semaphore()
-
-    def greet(i, carry):
-        pl.semaphore_signal(
-            barrier, inc=1, device_id={"tm": lax.rem(me + i, devices)},
-            device_id_type=pl.DeviceIdType.MESH,
-        )
-        return carry
-
-    lax.fori_loop(1, devices, greet, 0)
     pl.semaphore_wait(barrier, devices - 1)
 
     def copy(i):
@@ -228,32 +253,40 @@
     bins = phase_bins.reshape(samples // (2 * RADIX), 2 * RADIX)
     tables, twist = dft_tables()
     in_vmem = pl.BlockSpec(memory_space=pltpu.VMEM)
-    tiles = pl.pallas_call(
-        functools.partial(work_kernel, channels),
-        out_shape=jax.ShapeDtypeStruct((devices, 8, RADIX), F32),
+    gain, part, onehot = pl.pallas_call(
+        functools.partial(prep_kernel, channels),
+        out_shape=[
+            jax.ShapeDtypeStruct((channels, RADIX, 2 * RADIX), F32),
+            jax.ShapeDtypeStruct((channels, 2 * RADIX, 2 * RADIX), F32),
+            jax.ShapeDtypeStruct((LOW_BINS, samples), BF16),
+        ],
+        in_specs=[in_vmem] * 4,
+        out_specs=[in_vmem] * 3,
+        compiler_params=pltpu.CompilerParams(vmem_limit_bytes=24 * 2**20),
+        cost_estimate=pl.CostEstimate(
+            flops=4 * 10**9, bytes_accessed=9 * 2**20, transcendentals=0
+        ),
+        name="prep",
+    )(cur, chirp, bins, tables[1])
+    factor = 1.0 / float(samples * devices // BINS)
+    return pl.pallas_call(
+        functools.partial(work_kernel, channels, devices, factor),
+        out_shape=jax.ShapeDtypeStruct((channels, 4, BINS // devices), F32),
         in_specs=[in_vmem] * 13,
         out_specs=in_vmem,
         scratch_shapes=[
             pltpu.VMEM((HALF * rows, RADIX), F32),
             pltpu.VMEM((8 * rows, samples), BF16),
-            pltpu.VMEM((LOW_BINS, samples), BF16),
-        ],
-        name="work",
-    )(prev, cur, chirp, bins, *tables, twist)
-    factor = 1.0 / float(samples * devices // BINS)
-    return pl.pallas_call(
-        functools.partial(sum_kernel, devices, factor),
-        out_shape=jax.ShapeDtypeStruct((channels, 4, BINS // devices), F32),
-        in_specs=[in_vmem],
-        out_specs=in_vmem,
-        scratch_shapes=[
+            pltpu.VMEM((devices, 8, RADIX), F32),
             pltpu.VMEM((devices, 8, RADIX), F32),
             pltpu.SemaphoreType.DMA((devices,)),
             pltpu.SemaphoreType.DMA((devices,)),
         ],
-        compiler_params=pltpu.CompilerParams(collective_id=0, has_side_effects=True),
-        name="sum",
-    )(tiles)
+        compiler_params=pltpu.CompilerParams(
+            collective_id=0, has_side_effects=True, vmem_limit_bytes=32 * 2**20
+        ),
+        name="work",
+    )(prev, gain, part, onehot, bins, tables[0], *tables[2:], twist)
 
 
 def solution(mesh):

time: 62.6 us -> 48.1 us (0.77)
  Pallas kernels: 47.8 us -> 37.5 us
  waiting for transfers between devices: 4.56 us -> 0.55 us
    pallas_call x2, Pallas kernels: 47.8 us -> 37.5 us  [the longest x1 34.8 us: shards(): pl.pallas_call(functools.partial(work_kernel, channels, devices, factor),...]
    ppermute x1, waiting for transfers between devices: 4.56 us -> 0.55 us  [shards(): prev = lax.ppermute(cur, 'tm', [(i, i + 1) for i in range(devices - 1)])]
    unnamed x10 -> x20, local copies, waits for them, and re-layouts: 3.04 us -> 2.7 us
  transfers between devices with their start and end apart: 1 -> 1, of which waited for: 1 -> 1; matrix products, arithmetic and copies ran while one was open for 2% -> 4% of each run, Pallas kernels for 0% -> 6%
where the time goes in v2:
time: 48.1 us; the launch traced here: 47.8 us
  Pallas kernels  37.5 us (78%)
  local copies, waits for them, and re-layouts  5.05 us (10%)
  starting transfers between devices  4.58 us (10%)
  waiting for transfers between devices  0.55 us (1%)
    pallas_call x1, Pallas kernels, shards(): pl.pallas_call(functools.partial(work_kernel, channels, devices, factor),...  34.8 us
    ppermute x1, starting transfers between devices, shards(): prev = lax.ppermute(cur, 'tm', [(i, i + 1) for i in range(devices - 1)])  4.58 us
    unnamed x20, local copies, waits for them, and re-layouts  2.7 us
    pallas_call x1, Pallas kernels, shards(): pl.pallas_call(functools.partial(prep_kernel, channels), out_shape=[jax.S...  2.65 us
    reshape x1, local copies, waits for them, and re-layouts, shards(): cur = baseband.reshape(rows, HALF, RADIX)  1.58 us
  transfers between devices with their start and end apart: 1, of which 1 were waited for; matrix products, arithmetic and copies ran while one was open for 4% of the time, Pallas kernels for 6%

profile of v2, /device:TPU:1, one launch (start us, length us, event | category | flops | bytes accessed | tf_op | source)
XLA Modules:
  0.0 47.8 jit_solution(3962014337881616788)
XLA Ops:
  0.0 1.6 %reshape.9.cur = bf16[32,64,128]{2,1,0:T(8,128)(2,1)S(1)} reshape(bf16[8,4,8192]{2,1,0:T(4,128)(2,1)} %param.12) | data formatting | bytes 1048576 | tf_op jit(solution)/shard_map/reshape | solution.py:250
  1.6 4.6 %collective-permute-start = (bf16[32,64,128]{2,1,0:T(8,128)(2,1)S(1)}, bf16[32,64,128]{2,1,0:T(8,128)(2,1)S(1)}, u32[]{:S(2)}, u32[]{:S(2)}) collective-permute-start(bf16[32,64,128]{2,1,0:T(8,128)(2,1)S(1)} %reshape.9.cur), channel_id=1, source_target_pairs={{0,1},{1,2},{2,3},{3,4},{4,5},{5,6},{6,7},{7,8},{8,9},{9,10},{10,1... | collective-permute-start | bytes 1572872 | tf_op jit(solution)/shard_map/ppermute | solution.py:251
  6.2 0.8 %reshape.11.bins = s32[32,256]{1,0:T(8,128)S(1)} reshape(s32[8192]{0:T(1024)} %param.14) | data formatting | bytes 65536 | tf_op jit(solution)/shard_map/reshape | solution.py:253
  6.9 1.1 %copy.15 = f32[1,8,128,128]{3,2,1,0:T(8,128)S(1)} copy(f32[1,8,128,128]{3,1,2,0:T(8,128)} %bitcast.5) | data formatting | bytes 1048576
  8.1 0.0 copy-start.8
  8.1 0.9 %copy-done.8 = bf16[256,256]{1,0:T(8,128)(2,1)S(1)} copy-done((bf16[256,256]{1,0:T(8,128)(2,1)S(1)}, bf16[256,256]{1,0:T(8,128)(2,1)}, u32[]{:S(2)}) %copy-start.8) | copy-done | bytes 131096
  9.0 0.0 copy-start
  9.0 0.0 copy-start.1
  9.0 0.0 copy-start.2
  9.0 0.0 copy-start.3
  9.0 0.0 copy-start.4
  9.0 0.0 copy-start.5
  9.0 0.0 copy-start.6
  9.1 0.0 copy-start.7
  9.1 2.7 %prep.1 = (f32[8,128,256]{2,1,0:T(8,128)S(1)}, f32[8,256,256]{2,1,0:T(8,128)S(1)}, bf16[256,8192]{1,0:T(8,128)(2,1)S(1)}) custom-call(bf16[32,64,128]{2,1,0:T(8,128)(2,1)S(1)} %reshape.9.cur, f32[8,128,128]{2,1,0:T(8,128)S(1)} %bitcast.4, s32[32,256]{1,0:T(8,128)S(1)} %reshape.11.bins, bf16[256,256]{1,0:T(8,128)(2,1)S(1)} %copy-done.8), custom_call_target="tpu_custom_call" | custom-call | flops 4000000000 | bytes 9437184 | tf_op jit(solution)/shard_map/prep/pallas_call | solution.py:256
  11.7 0.6 %collective-permute-done.prev = bf16[32,64,128]{2,1,0:T(8,128)(2,1)S(1)} collective-permute-done((bf16[32,64,128]{2,1,0:T(8,128)(2,1)S(1)}, bf16[32,64,128]{2,1,0:T(8,128)(2,1)S(1)}, u32[]{:S(2)}, u32[]{:S(2)}) %collective-permute-start) | collective-permute-done | bytes 524320 | tf_op jit(solution)/shard_map/ppermute | solution.py:251
  12.3 0.0 copy-done
  12.3 0.0 copy-done.1
  12.3 0.0 copy-done.2
  12.3 0.0 copy-done.3
  12.3 0.0 copy-done.4
  12.3 0.0 copy-done.5
  12.3 0.0 copy-done.6
  12.3 0.0 copy-done.7
  12.3 34.8 %work.1 = f32[8,4,32]{2,1,0:T(4,128)S(1)} custom-call(bf16[32,64,128]{2,1,0:T(8,128)(2,1)S(1)} %collective-permute-done.prev, f32[8,128,256]{2,1,0:T(8,128)S(1)} %get-tuple-element.8.gain, f32[8,256,256]{2,1,0:T(8,128)S(1)} %get-tuple-element.9.part, bf16[256,8192]{1,0:T(8,128)(2,1)S(1)} %get-tuple-element.10.onehot, s32[32,256]{1,0:T(8,128)S(1)} %reshape.11.bins, ...), custom_call_target="tpu_custom_call" | custom-call | tf_op jit(solution)/shard_map/work/pallas_call | solution.py:272
  47.2 0.6 %copy.17 = f32[8,4,32]{2,1,0:T(4,128)} copy(f32[8,4,32]{2,1,0:T(4,128)S(1)} %work.1) | data formatting | bytes 8192
Async XLA Ops:
  1.6 10.7 %collective-permute-start = (bf16[32,64,128]{2,1,0:T(8,128)(2,1)S(1)}, bf16[32,64,128]{2,1,0:T(8,128)(2,1)S(1)}, u32[]{:S(2)}, u32[]{:S(2)}) collective-permute-start(bf16[32,64,128]{2,1,0:T(8,128)(2,1)S(1)} %reshape.9.cur), channel_id=1, source_target_pairs={{0,1},{1,2},{2,3},{3,4},{4,5},{5,6},{6,7},{7,8},{8,9},{9,10},{10,1... | collective-permute-start | bytes 1572872 | tf_op jit(solution)/shard_map/ppermute | solution.py:251
  8.1 0.9 %copy-start.8 = (bf16[256,256]{1,0:T(8,128)(2,1)S(1)}, bf16[256,256]{1,0:T(8,128)(2,1)}, u32[]{:S(2)}) copy-start(bf16[256,256]{1,0:T(8,128)(2,1)} %constant.18.clone.left) | copy-start | bytes 393220
  9.0 3.3 %copy-start = (bf16[256,256]{1,0:T(8,128)(2,1)S(1)}, bf16[256,256]{1,0:T(8,128)(2,1)}, u32[]{:S(2)}) copy-start(bf16[256,256]{1,0:T(8,128)(2,1)} %constant.19.clone.left) | copy-start | bytes 393220
  9.0 3.3 %copy-start.1 = (bf16[256,256]{1,0:T(8,128)(2,1)S(1)}, bf16[256,256]{1,0:T(8,128)(2,1)}, u32[]{:S(2)}) copy-start(bf16[256,256]{1,0:T(8,128)(2,1)} %constant.20.clone.right_h) | copy-start | bytes 393220
  9.0 3.3 %copy-start.2 = (bf16[256,256]{1,0:T(8,128)(2,1)S(1)}, bf16[256,256]{1,0:T(8,128)(2,1)}, u32[]{:S(2)}) copy-start(bf16[256,256]{1,0:T(8,128)(2,1)} %constant.21.clone.right_l) | copy-start | bytes 393220
  9.0 3.3 %copy-start.3 = (bf16[256,256]{1,0:T(8,128)(2,1)S(1)}, bf16[256,256]{1,0:T(8,128)(2,1)}, u32[]{:S(2)}) copy-start(bf16[256,256]{1,0:T(8,128)(2,1)} %constant.22.clone.back_right_h) | copy-start | bytes 393220
  9.0 3.3 %copy-start.4 = (bf16[256,256]{1,0:T(8,128)(2,1)S(1)}, bf16[256,256]{1,0:T(8,128)(2,1)}, u32[]{:S(2)}) copy-start(bf16[256,256]{1,0:T(8,128)(2,1)} %constant.23.clone.back_right_l) | copy-start | bytes 393220
  9.0 3.3 %copy-start.5 = (f32[128,256]{1,0:T(8,128)S(1)}, f32[128,256]{1,0:T(8,128)}, u32[]{:S(2)}) copy-start(f32[128,256]{1,0:T(8,128)} %constant.26.clone.twist) | copy-start | bytes 393220
  9.0 3.3 %copy-start.6 = (bf16[128,256]{1,0:T(8,128)(2,1)S(1)}, bf16[128,256]{1,0:T(8,128)(2,1)}, u32[]{:S(2)}) copy-start(bf16[128,256]{1,0:T(8,128)(2,1)} %constant.24.clone.back_left_h) | copy-start | bytes 196612
  9.1 3.3 %copy-start.7 = (bf16[128,256]{1,0:T(8,128)(2,1)S(1)}, bf16[128,256]{1,0:T(8,128)(2,1)}, u32[]{:S(2)}) copy-start(bf16[128,256]{1,0:T(8,128)(2,1)} %constant.25.clone.back_left_l) | copy-start | bytes 196612

commit v3 on v2

--- a/solution.py
+++ b/solution.py
@@ -75,16 +75,20 @@
     return dot(table[...], jnp.concatenate([series, series], axis=0))
 
 
-def prep_kernel(channels, cur, chirp, bins, left, gain, part, onehot):
+def prep_kernel(sizes, *refs):
+    curs, (chirp, bins, left, gain, part, onehot) = refs[:len(sizes)], refs[len(sizes):]
     lane_bins = lax.broadcasted_iota(jnp.int32, (LOW_BINS, 2 * RADIX), 0)
 
-    def channel(c, carry):
-        cosine, sine = cos_sin(chirp[c].T)
-        gain[c] = jnp.concatenate([cosine, sine], axis=1)
-        part[c] = first_stage(left, cur, 4 * c)
-        return carry
-
-    lax.fori_loop(0, channels, channel, 0)
+    for chunk, cur in enumerate(curs):
+        start = sum(sizes[:chunk])
+
+        def channel(c, carry):
+            cosine, sine = cos_sin(chirp[start + c].T)
+            gain[start + c] = jnp.concatenate([cosine, sine], axis=1)
+            part[start + c] = first_stage(left, cur, 4 * c)
+            return carry
+
+        lax.fori_loop(0, sizes[chunk], channel, 0)
 
     def mark(m, carry):
         own = bins[pl.ds(m, 1), :]
@@ -97,24 +101,11 @@
     lax.fori_loop(0, HALF // 2, mark, 0)
 
 
-def work_kernel(
-    channels, devices, factor, prev, gain, part, onehot, bins, left, right_h, right_l,
-    back_right_h, back_right_l, back_left_h, back_left_l, twist, out, stokes, picked, tiles,
-    landed, send_sems, recv_sems,
+def filter_channels(
+    start, size, prev, gain, part, left, right_h, right_l, back_right_h, back_right_l,
+    back_left_h, back_left_l, twist, stokes,
 ):
-    me = lax.axis_index("tm")
-    barrier = pltpu.get_barrier_semaphore()
-
-    def greet(i, carry):
-        pl.semaphore_signal(
-            barrier, inc=1, device_id={"tm": lax.rem(me + i, devices)},
-            device_id_type=pl.DeviceIdType.MESH,
-        )
-        return carry
-
-    lax.fori_loop(1, devices, greet, 0)
-
-    rows = 4 * channels
+    rows = 4 * size
     twist_real = twist[:, :RADIX]
     twist_imag = twist[:, RADIX:]
     wide_real = jnp.concatenate([twist_real, twist_real], axis=1)
@@ -122,11 +113,11 @@
 
     def channel(c):
         base = 4 * c
-        section = part[c] + first_stage(left, prev, base)
+        section = part[start + c] + first_stage(left, prev, base)
         real, imag = section[:RADIX], section[RADIX:]
         turned_real = real * wide_real - imag * wide_imag
         turned_imag = real * wide_imag + imag * wide_real
-        gain_real, gain_imag = gain[c, :, :RADIX], gain[c, :, RADIX:]
+        gain_real, gain_imag = gain[start + c, :, :RADIX], gain[start + c, :, RADIX:]
         waves_real, waves_imag = [], []
         for p in range(2):
             lanes = slice(p * RADIX, (p + 1) * RADIX)
@@ -174,15 +165,42 @@
         channel(2 * i + 1)
         return carry
 
-    lax.fori_loop(0, channels // 2, channel_pair, 0)
-
+    lax.fori_loop(0, size // 2, channel_pair, 0)
+
+
+def work_kernel(sizes, devices, factor, *refs):
+    ready, refs = refs[:len(sizes) - 1], refs[len(sizes) - 1:]
+    onehot, bins, *operands = refs[:13]
+    out, last, picked, tiles, landed, send_sems, recv_sems = refs[13:]
+    me = lax.axis_index("tm")
+    barrier = pltpu.get_barrier_semaphore()
+
+    def greet(i, carry):
+        pl.semaphore_signal(
+            barrier, inc=1, device_id={"tm": lax.rem(me + i, devices)},
+            device_id_type=pl.DeviceIdType.MESH,
+        )
+        return carry
+
+    lax.fori_loop(1, devices, greet, 0)
+
+    start = sum(sizes[:-1])
+    filter_channels(start, sizes[-1], *operands, last)
+    stokes = (*ready, last)
+    rows = 4 * sum(sizes)
     groups = BINS // LOW_BINS
 
     def pick(m, carry):
-        start = pl.multiple_of(m * 2 * rows, 2 * rows)
-        value = jnp.concatenate(
-            [stokes[pl.ds(start, rows), :], stokes[pl.ds(start + rows, rows), :]], axis=1
-        )
+        pieces = []
+        for array, size in zip(stokes, sizes):
+            count = 4 * size
+            at = pl.multiple_of(m * 2 * count, 2 * count)
+            pieces.append(
+                jnp.concatenate(
+                    [array[pl.ds(at, count), :], array[pl.ds(at + count, count), :]], axis=1
+                )
+            )
+        value = jnp.concatenate(pieces, axis=0)
         high = value.astype(BF16).astype(F32)
         both = jnp.concatenate([high, value - high], axis=0)
         group = bins[pl.ds(m, 1), :] // LOW_BINS
@@ -247,35 +265,57 @@
     channels, _, samples = baseband.shape
     devices = lax.axis_size("tm")
     rows = 4 * channels
-    cur = baseband.reshape(rows, HALF, RADIX)
-    prev = lax.ppermute(cur, "tm", [(i, i + 1) for i in range(devices - 1)])
+    sizes = (channels // 2, channels // 4, channels // 4)
+    route = [(i, i + 1) for i in range(devices - 1)]
+    curs, prevs = [], []
+    for chunk, size in enumerate(sizes):
+        start = sum(sizes[:chunk])
+        cur = baseband[start:start + size].reshape(4 * size, HALF, RADIX)
+        curs.append(cur)
+        prevs.append(lax.ppermute(cur, "tm", route))
     chirp = chirp_phase.reshape(channels, RADIX, RADIX)
     bins = phase_bins.reshape(samples // (2 * RADIX), 2 * RADIX)
     tables, twist = dft_tables()
     in_vmem = pl.BlockSpec(memory_space=pltpu.VMEM)
     gain, part, onehot = pl.pallas_call(
-        functools.partial(prep_kernel, channels),
+        functools.partial(prep_kernel, sizes),
         out_shape=[
             jax.ShapeDtypeStruct((channels, RADIX, 2 * RADIX), F32),
             jax.ShapeDtypeStruct((channels, 2 * RADIX, 2 * RADIX), F32),
             jax.ShapeDtypeStruct((LOW_BINS, samples), BF16),
         ],
-        in_specs=[in_vmem] * 4,
+        in_specs=[in_vmem] * (len(sizes) + 3),
         out_specs=[in_vmem] * 3,
         compiler_params=pltpu.CompilerParams(vmem_limit_bytes=24 * 2**20),
         cost_estimate=pl.CostEstimate(
             flops=4 * 10**9, bytes_accessed=9 * 2**20, transcendentals=0
         ),
         name="prep",
-    )(cur, chirp, bins, tables[1])
+    )(*curs, chirp, bins, tables[1])
+    constants = (tables[0], *tables[2:], twist)
+    ready = []
+    for chunk, size in enumerate(sizes[:-1]):
+        ready.append(
+            pl.pallas_call(
+                functools.partial(filter_channels, sum(sizes[:chunk]), size),
+                out_shape=jax.ShapeDtypeStruct((HALF * 4 * size, RADIX), F32),
+                in_specs=[in_vmem] * 11,
+                out_specs=in_vmem,
+                compiler_params=pltpu.CompilerParams(vmem_limit_bytes=24 * 2**20),
+                cost_estimate=pl.CostEstimate(
+                    flops=size * 10**9, bytes_accessed=size * 2**20, transcendentals=0
+                ),
+                name="filter",
+            )(prevs[chunk], gain, part, *constants)
+        )
     factor = 1.0 / float(samples * devices // BINS)
     return pl.pallas_call(
-        functools.partial(work_kernel, channels, devices, factor),
+        functools.partial(work_kernel, sizes, devices, factor),
         out_shape=jax.ShapeDtypeStruct((channels, 4, BINS // devices), F32),
-        in_specs=[in_vmem] * 13,
+        in_specs=[in_vmem] * (len(ready) + 13),
         out_specs=in_vmem,
         scratch_shapes=[
-            pltpu.VMEM((HALF * rows, RADIX), F32),
+            pltpu.VMEM((HALF * 4 * sizes[-1], RADIX), F32),
             pltpu.VMEM((8 * rows, samples), BF16),
             pltpu.VMEM((devices, 8, RADIX), F32),
             pltpu.VMEM((devices, 8, RADIX), F32),
@@ -286,7 +326,7 @@
             collective_id=0, has_side_effects=True, vmem_limit_bytes=32 * 2**20
         ),
         name="work",
-    )(prev, gain, part, onehot, bins, tables[0], *tables[2:], twist)
+    )(*ready, onehot, bins, prevs[-1], gain, part, *constants)
 
 
 def solution(mesh):

time: 48.1 us -> 46.4 us (0.965)
  Pallas kernels: 37.5 us -> 29.6 us
  starting transfers between devices: 4.58 us -> 10.1 us
  local copies, waits for them, and re-layouts: 5.05 us -> 6.16 us
  waiting for transfers between devices: 0.55 us -> 0.01 us
    pallas_call x2 -> x4, Pallas kernels: 37.5 us -> 29.6 us  [the longest x1 22.1 us: shards(): pl.pallas_call(functools.partial(work_kernel, sizes, devices, factor), ou...]
    ppermute x1 -> x3, starting transfers between devices: 4.58 us -> 10.1 us  [shards(): prevs.append(lax.ppermute(cur, 'tm', route))]
    slice x0 -> x2, local copies, waits for them, and re-layouts: none -> 2.1 us  [shards(): cur = baseband[start:start + size].reshape(4 * size, HALF, RADIX)]
    reshape x1 -> x3, local copies, waits for them, and re-layouts: 1.58 us -> 0.59 us  [shards(): cur = baseband[start:start + size].reshape(4 * size, HALF, RADIX)]
    ppermute x1 -> x3, waiting for transfers between devices: 0.55 us -> 0.01 us  [shards(): prevs.append(lax.ppermute(cur, 'tm', route))]
  transfers between devices with their start and end apart: 1 -> 3, of which waited for: 1 -> 0; matrix products, arithmetic and copies ran while one was open for 4% -> 7% of each run, Pallas kernels for 6% -> 16%
where the time goes in v3:
time: 46.4 us; the launch traced here: 46.1 us
  Pallas kernels  29.6 us (64%)
  starting transfers between devices  10.1 us (22%)
  local copies, waits for them, and re-layouts  6.16 us (13%)
    pallas_call x1, Pallas kernels, shards(): pl.pallas_call(functools.partial(work_kernel, sizes, devices, factor), ou...  22.1 us
    ppermute x3, starting transfers between devices, shards(): prevs.append(lax.ppermute(cur, 'tm', route))  10.1 us
    pallas_call x2, Pallas kernels, shards(): pl.pallas_call(functools.partial(filter_channels, sum(sizes[:chunk]), siz...  4.86 us
    unnamed x20, local copies, waits for them, and re-layouts  2.7 us
    pallas_call x1, Pallas kernels, shards(): pl.pallas_call(functools.partial(prep_kernel, sizes), out_shape=[jax.Shap...  2.65 us
    slice x2, local copies, waits for them, and re-layouts, shards(): cur = baseband[start:start + size].reshape(4 * size, HALF, RADIX)  2.1 us
  transfers between devices with their start and end apart: 3, of which 0 were waited for; matrix products, arithmetic and copies ran while one was open for 7% of the time, Pallas kernels for 16%

profile of v3, /device:TPU:1, one launch (start us, length us, event | category | flops | bytes accessed | tf_op | source)
XLA Modules:
  0.0 46.1 jit_solution(512882406454597086)
XLA Ops:
  0.0 1.1 %fusion = (bf16[2,4,8192]{2,1,0:T(4,128)(2,1)S(1)}, bf16[2,4,8192]{2,1,0:T(4,128)(2,1)S(1)}) fusion(bf16[8,4,8192]{2,1,0:T(4,128)(2,1)} %param.12), kind=kLoop, calls=%fused_computation.1 | loop fusion | bytes 524288 | tf_op jit(solution)/shard_map/slice | solution.py:273
  1.1 0.2 reshape.16.refs_1_
  1.2 4.6 %collective-permute-start.1 = (bf16[8,64,128]{2,1,0:T(8,128)(2,1)S(1)}, bf16[8,64,128]{2,1,0:T(8,128)(2,1)S(1)}, u32[]{:S(2)}, u32[]{:S(2)}) collective-permute-start(bf16[8,64,128]{2,1,0:T(8,128)(2,1)S(1)} %reshape.16.refs_1_), channel_id=1, source_target_pairs={{0,1},{1,2},{2,3},{3,4},{4,5},{5,6},{6,7},{7,8},{8,9},{9,10},{10,1... | collective-permute-start | bytes 393224 | tf_op jit(solution)/shard_map/ppermute | solution.py:275
  5.8 1.0 %slice.9 = bf16[4,4,8192]{2,1,0:T(4,128)(2,1)S(1)} slice(bf16[8,4,8192]{2,1,0:T(4,128)(2,1)} %param.12), slice={[0:4], [0:4], [0:8192]} | slice | bytes 524288 | tf_op jit(solution)/shard_map/slice | solution.py:273
  6.9 0.3 reshape.15.refs_0_
  7.2 1.9 %collective-permute-start = (bf16[16,64,128]{2,1,0:T(8,128)(2,1)S(1)}, bf16[16,64,128]{2,1,0:T(8,128)(2,1)S(1)}, u32[]{:S(2)}, u32[]{:S(2)}) collective-permute-start(bf16[16,64,128]{2,1,0:T(8,128)(2,1)S(1)} %reshape.15.refs_0_), channel_id=1, source_target_pairs={{0,1},{1,2},{2,3},{3,4},{4,5},{5,6},{6,7},{7,8},{8,9},{9,10},{10,1... | collective-permute-start | bytes 786440 | tf_op jit(solution)/shard_map/ppermute | solution.py:275
  9.1 0.2 reshape.17.refs_2_
  9.2 3.6 %collective-permute-start.2 = (bf16[8,64,128]{2,1,0:T(8,128)(2,1)S(1)}, bf16[8,64,128]{2,1,0:T(8,128)(2,1)S(1)}, u32[]{:S(2)}, u32[]{:S(2)}) collective-permute-start(bf16[8,64,128]{2,1,0:T(8,128)(2,1)S(1)} %reshape.17.refs_2_), channel_id=1, source_target_pairs={{0,1},{1,2},{2,3},{3,4},{4,5},{5,6},{6,7},{7,8},{8,9},{9,10},{10,1... | collective-permute-start | bytes 393224 | tf_op jit(solution)/shard_map/ppermute | solution.py:275
  12.8 0.8 %reshape.19.refs_4_.refs_3_ = s32[32,256]{1,0:T(8,128)S(1)} reshape(s32[8192]{0:T(1024)} %param.14) | data formatting | bytes 65536 | tf_op jit(solution)/shard_map/reshape | solution.py:277
  13.6 1.1 %copy.15 = f32[1,8,128,128]{3,2,1,0:T(8,128)S(1)} copy(f32[1,8,128,128]{3,1,2,0:T(8,128)} %bitcast.5) | data formatting | bytes 1048576
  14.8 0.0 copy-start.8
  14.8 0.9 %copy-done.8 = bf16[256,256]{1,0:T(8,128)(2,1)S(1)} copy-done((bf16[256,256]{1,0:T(8,128)(2,1)S(1)}, bf16[256,256]{1,0:T(8,128)(2,1)}, u32[]{:S(2)}) %copy-start.8) | copy-done | bytes 131096
  15.7 0.0 copy-start.4
  15.7 0.0 copy-start.5
  15.7 0.0 copy-start.6
  15.7 0.0 copy-start.7
  15.7 2.6 %prep.1 = (f32[8,128,256]{2,1,0:T(8,128)S(1)}, f32[8,256,256]{2,1,0:T(8,128)S(1)}, bf16[256,8192]{1,0:T(8,128)(2,1)S(1)}) custom-call(bf16[16,64,128]{2,1,0:T(8,128)(2,1)S(1)} %reshape.15.refs_0_, bf16[8,64,128]{2,1,0:T(8,128)(2,1)S(1)} %reshape.16.refs_1_, bf16[8,64,128]{2,1,0:T(8,128)(2,1)S(1)} %reshape.17.refs_2_, f32[8,128,128]{2,1,0:T(8,128)S(1)} %bitcast.4, ...), custom_call_target="tpu_custom_call" | custom-call | flops 4000000000 | bytes 9437184 | tf_op jit(solution)/shard_map/prep/pallas_call | solution.py:280
  18.4 0.0 collective-permute-done.1.prev
  18.4 0.0 copy-done
  18.4 0.0 copy-done.1
  18.4 0.0 copy-done.2
  18.4 0.0 copy-done.3
  18.4 0.0 copy-done.4
  18.5 0.0 copy-done.5
  18.5 0.0 copy-done.6
  18.5 0.0 copy-done.7
  18.5 1.6 %filter.3.refs_1_ = f32[512,128]{1,0:T(8,128)S(1)} custom-call(bf16[8,64,128]{2,1,0:T(8,128)(2,1)S(1)} %collective-permute-done.1.prev, f32[8,128,256]{2,1,0:T(8,128)S(1)} %get-tuple-element.8.gain.refs_5_, f32[8,256,256]{2,1,0:T(8,128)S(1)} %get-tuple-element.9.part.refs_6_, bf16[256,256]{1,0:T(8,128)(2,1)S(1)} %copy-done, bf16[256,256]{1,0:T(8,128)(2,1)S(1)} %copy-done.1, ...), custom_call_target="tpu_custom_call" | custom-call | flops 2000000000 | bytes 2097152 | tf_op jit(solution)/shard_map/filter/pallas_call | solution.py:299
  20.1 0.0 collective-permute-done.prev
  20.1 3.3 %filter.2.refs_0_ = f32[1024,128]{1,0:T(8,128)S(1)} custom-call(bf16[16,64,128]{2,1,0:T(8,128)(2,1)S(1)} %collective-permute-done.prev, f32[8,128,256]{2,1,0:T(8,128)S(1)} %get-tuple-element.8.gain.refs_5_, f32[8,256,256]{2,1,0:T(8,128)S(1)} %get-tuple-element.9.part.refs_6_, bf16[256,256]{1,0:T(8,128)(2,1)S(1)} %copy-done, bf16[256,256]{1,0:T(8,128)(2,1)S(1)} %copy-done.1, ...), custom_call_target="tpu_custom_call" | custom-call | flops 4000000000 | bytes 4194304 | tf_op jit(solution)/shard_map/filter/pallas_call | solution.py:299
  23.4 0.0 collective-permute-done.2.refs_4_
  23.4 22.1 %work.1 = f32[8,4,32]{2,1,0:T(4,128)S(1)} custom-call(f32[1024,128]{1,0:T(8,128)S(1)} %filter.2.refs_0_, f32[512,128]{1,0:T(8,128)S(1)} %filter.3.refs_1_, bf16[256,8192]{1,0:T(8,128)(2,1)S(1)} %get-tuple-element.10.refs_2_, s32[32,256]{1,0:T(8,128)S(1)} %reshape.19.refs_4_.refs_3_, bf16[8,64,128]{2,1,0:T(8,128)(2,1)S(1)} %collective-permute-done.2.refs_4_, ...), custom_call_target="tpu_custom_call" | custom-call | tf_op jit(solution)/shard_map/work/pallas_call | solution.py:312
  45.4 0.6 %copy.17 = f32[8,4,32]{2,1,0:T(4,128)} copy(f32[8,4,32]{2,1,0:T(4,128)S(1)} %work.1) | data formatting | bytes 8192
  (4 shorter events, 0.0 us)
Async XLA Ops:
  1.2 17.2 %collective-permute-start.1 = (bf16[8,64,128]{2,1,0:T(8,128)(2,1)S(1)}, bf16[8,64,128]{2,1,0:T(8,128)(2,1)S(1)}, u32[]{:S(2)}, u32[]{:S(2)}) collective-permute-start(bf16[8,64,128]{2,1,0:T(8,128)(2,1)S(1)} %reshape.16.refs_1_), channel_id=1, source_target_pairs={{0,1},{1,2},{2,3},{3,4},{4,5},{5,6},{6,7},{7,8},{8,9},{9,10},{10,1... | collective-permute-start | bytes 393224 | tf_op jit(solution)/shard_map/ppermute | solution.py:275
  7.2 12.9 %collective-permute-start = (bf16[16,64,128]{2,1,0:T(8,128)(2,1)S(1)}, bf16[16,64,128]{2,1,0:T(8,128)(2,1)S(1)}, u32[]{:S(2)}, u32[]{:S(2)}) collective-permute-start(bf16[16,64,128]{2,1,0:T(8,128)(2,1)S(1)} %reshape.15.refs_0_), channel_id=1, source_target_pairs={{0,1},{1,2},{2,3},{3,4},{4,5},{5,6},{6,7},{7,8},{8,9},{9,10},{10,1... | collective-permute-start | bytes 786440 | tf_op jit(solution)/shard_map/ppermute | solution.py:275
  9.2 14.1 %collective-permute-start.2 = (bf16[8,64,128]{2,1,0:T(8,128)(2,1)S(1)}, bf16[8,64,128]{2,1,0:T(8,128)(2,1)S(1)}, u32[]{:S(2)}, u32[]{:S(2)}) collective-permute-start(bf16[8,64,128]{2,1,0:T(8,128)(2,1)S(1)} %reshape.17.refs_2_), channel_id=1, source_target_pairs={{0,1},{1,2},{2,3},{3,4},{4,5},{5,6},{6,7},{7,8},{8,9},{9,10},{10,1... | collective-permute-start | bytes 393224 | tf_op jit(solution)/shard_map/ppermute | solution.py:275
  14.8 0.9 %copy-start.8 = (bf16[256,256]{1,0:T(8,128)(2,1)S(1)}, bf16[256,256]{1,0:T(8,128)(2,1)}, u32[]{:S(2)}) copy-start(bf16[256,256]{1,0:T(8,128)(2,1)} %constant.18.clone.refs_5_) | copy-start | bytes 393220
  15.7 2.7 %copy-start = (bf16[256,256]{1,0:T(8,128)(2,1)S(1)}, bf16[256,256]{1,0:T(8,128)(2,1)}, u32[]{:S(2)}) copy-start(bf16[256,256]{1,0:T(8,128)(2,1)} %constant.19.clone.left.refs_7_) | copy-start | bytes 393220
  15.7 2.7 %copy-start.1 = (bf16[256,256]{1,0:T(8,128)(2,1)S(1)}, bf16[256,256]{1,0:T(8,128)(2,1)}, u32[]{:S(2)}) copy-start(bf16[256,256]{1,0:T(8,128)(2,1)} %constant.20.clone.right_h.refs_8_) | copy-start | bytes 393220
  15.7 2.7 %copy-start.2 = (bf16[256,256]{1,0:T(8,128)(2,1)S(1)}, bf16[256,256]{1,0:T(8,128)(2,1)}, u32[]{:S(2)}) copy-start(bf16[256,256]{1,0:T(8,128)(2,1)} %constant.21.clone.right_l.refs_9_) | copy-start | bytes 393220
  15.7 2.8 %copy-start.3 = (bf16[256,256]{1,0:T(8,128)(2,1)S(1)}, bf16[256,256]{1,0:T(8,128)(2,1)}, u32[]{:S(2)}) copy-start(bf16[256,256]{1,0:T(8,128)(2,1)} %constant.22.clone.back_right_h.refs_10_) | copy-start | bytes 393220
  15.7 2.8 %copy-start.4 = (bf16[256,256]{1,0:T(8,128)(2,1)S(1)}, bf16[256,256]{1,0:T(8,128)(2,1)}, u32[]{:S(2)}) copy-start(bf16[256,256]{1,0:T(8,128)(2,1)} %constant.23.clone.back_right_l.refs_11_) | copy-start | bytes 393220
  15.7 2.8 %copy-start.5 = (f32[128,256]{1,0:T(8,128)S(1)}, f32[128,256]{1,0:T(8,128)}, u32[]{:S(2)}) copy-start(f32[128,256]{1,0:T(8,128)} %constant.26.clone.twist.refs_14_) | copy-start | bytes 393220
  15.7 2.8 %copy-start.6 = (bf16[128,256]{1,0:T(8,128)(2,1)S(1)}, bf16[128,256]{1,0:T(8,128)(2,1)}, u32[]{:S(2)}) copy-start(bf16[128,256]{1,0:T(8,128)(2,1)} %constant.24.clone.back_left_h.refs_12_) | copy-start | bytes 196612
  15.7 2.8 %copy-start.7 = (bf16[128,256]{1,0:T(8,128)(2,1)S(1)}, bf16[128,256]{1,0:T(8,128)(2,1)}, u32[]{:S(2)}) copy-start(bf16[128,256]{1,0:T(8,128)(2,1)} %constant.25.clone.back_left_l.refs_13_) | copy-start | bytes 196612

commit v4 on v3

--- a/solution.py
+++ b/solution.py
@@ -171,18 +171,34 @@
 def work_kernel(sizes, devices, factor, *refs):
     ready, refs = refs[:len(sizes) - 1], refs[len(sizes) - 1:]
     onehot, bins, *operands = refs[:13]
-    out, last, picked, tiles, landed, send_sems, recv_sems = refs[13:]
+    out, last, picked, tiles, swapped, sums, landed, *sems = refs[13:]
+    swap_sems, send_sems, recv_sems = sems
     me = lax.axis_index("tm")
     barrier = pltpu.get_barrier_semaphore()
 
-    def greet(i, carry):
+    chips = devices // 2
+    half = chips // 2
+    core, chip = lax.rem(me, 2), me // 2
+    side, place = chip // half, lax.rem(chip, half)
+    partner = me + 1 - 2 * core
+
+    def peer_chip(i):
+        other = lax.rem(side + 1 - i // half, 2)
+        return other * half + lax.rem(place + i, half)
+
+    def greet(device):
         pl.semaphore_signal(
-            barrier, inc=1, device_id={"tm": lax.rem(me + i, devices)},
-            device_id_type=pl.DeviceIdType.MESH,
-        )
-        return carry
-
-    lax.fori_loop(1, devices, greet, 0)
+            barrier, inc=1, device_id={"tm": device}, device_id_type=pl.DeviceIdType.MESH
+        )
+
+    def greet_chip(i, carry):
+        greet(peer_chip(i) * 2 + core)
+        return carry
+
+    steps = [(0, half), (half + 1, chips)]
+    for low, high in steps:
+        lax.fori_loop(low, high, greet_chip, 0)
+    greet(partner)
 
     start = sum(sizes[:-1])
     filter_channels(start, sizes[-1], *operands, last)
@@ -211,7 +227,7 @@
             ).astype(BF16)
         return carry
 
-    lax.fori_loop(0, HALF // 2, pick, 0)
+    lax.fori_loop(0, HALF // 2, pick, 0, unroll=4)
 
     total = lax.dot_general(
         picked[...], onehot[...], (((1,), (1,)), ((), ())), preferred_element_type=F32
@@ -222,50 +238,68 @@
         for h in range(2):
             for b in range(4):
                 lanes = slice(h * RADIX + 32 * b, h * RADIX + 32 * b + 32)
-                tiles[q * 8 + h * 4 + b] = jnp.concatenate(
+                tiles[b % 2, q * 4 + h * 2 + b // 2] = jnp.concatenate(
                     [folded[8 * a:8 * a + 8, lanes] for a in range(4)], axis=1
                 )
 
-    pl.semaphore_wait(barrier, devices - 1)
+    pl.semaphore_wait(barrier, chips)
+
+    swap = pltpu.make_async_remote_copy(
+        src_ref=tiles.at[1 - core],
+        dst_ref=swapped,
+        send_sem=swap_sems.at[0],
+        recv_sem=swap_sems.at[1],
+        device_id={"tm": partner},
+        device_id_type=pl.DeviceIdType.MESH,
+    )
+    swap.start()
+    swap.wait_recv()
+    sums[...] = tiles[core] + swapped[...]
 
     def copy(i):
-        peer = lax.rem(me + i, devices)
+        peer = peer_chip(i)
         return pltpu.make_async_remote_copy(
-            src_ref=tiles.at[peer],
+            src_ref=sums.at[peer],
             dst_ref=landed.at[i],
             send_sem=send_sems.at[i],
             recv_sem=recv_sems.at[i],
-            device_id={"tm": peer},
+            device_id={"tm": peer * 2 + core},
             device_id_type=pl.DeviceIdType.MESH,
         )
 
     def send(i, carry):
         copy(i).start()
         return carry
-
-    lax.fori_loop(1, devices, send, 0)
 
     def take(i, total):
         copy(i).wait_recv()
         return total + landed[i]
 
-    total = lax.fori_loop(1, devices, take, tiles[me]) * factor
+    for low, high in steps:
+        lax.fori_loop(low, high, send, 0)
+    total = sums[chip]
+    for low, high in reversed(steps):
+        total = lax.fori_loop(low, high, take, total)
+    total = total * factor
     for a in range(4):
         for k in range(2):
             out[2 * a + k] = total[4 * k:4 * k + 4, 32 * a:32 * a + 32]
 
+    swap.wait_send()
+
     def drain(i, carry):
         copy(i).wait_send()
         return carry
 
-    lax.fori_loop(1, devices, drain, 0)
+    for low, high in steps:
+        lax.fori_loop(low, high, drain, 0)
 
 
 def shards(baseband, chirp_phase, phase_bins):
     channels, _, samples = baseband.shape
     devices = lax.axis_size("tm")
     rows = 4 * channels
-    sizes = (channels // 2, channels // 4, channels // 4)
+    sizes = (channels // 2, channels // 2)
     route = [(i, i + 1) for i in range(devices - 1)]
     curs, prevs = [], []
     for chunk, size in enumerate(sizes):
@@ -317,10 +351,13 @@
         scratch_shapes=[
             pltpu.VMEM((HALF * 4 * sizes[-1], RADIX), F32),
             pltpu.VMEM((8 * rows, samples), BF16),
-            pltpu.VMEM((devices, 8, RADIX), F32),
-            pltpu.VMEM((devices, 8, RADIX), F32),
-            pltpu.SemaphoreType.DMA((devices,)),
-            pltpu.SemaphoreType.DMA((devices,)),
+            pltpu.VMEM((2, devices // 2, 8, RADIX), F32),
+            pltpu.VMEM((devices // 2, 8, RADIX), F32),
+            pltpu.VMEM((devices // 2, 8, RADIX), F32),
+            pltpu.VMEM((devices // 2, 8, RADIX), F32),
+            pltpu.SemaphoreType.DMA((2,)),
+            pltpu.SemaphoreType.DMA((devices // 2,)),
+            pltpu.SemaphoreType.DMA((devices // 2,)),
         ],
         compiler_params=pltpu.CompilerParams(
             collective_id=0, has_side_effects=True, vmem_limit_bytes=32 * 2**20

time: 46.4 us -> 44 us (0.948)
  starting transfers between devices: 10.1 us -> 6.5 us
  Pallas kernels: 29.6 us -> 31.7 us
  local copies, waits for them, and re-layouts: 6.16 us -> 5.24 us
    pallas_call x1, Pallas kernels: 22.1 us -> 25.8 us  [shards(): pl.pallas_call(functools.partial(work_kernel, sizes, devices, factor), ou...]
    ppermute x3 -> x2, starting transfers between devices: 10.1 us -> 6.5 us  [shards(): prevs.append(lax.ppermute(cur, 'tm', route))]
    pallas_call x2 -> x1, Pallas kernels: 4.86 us -> 3.26 us  [shards(): pl.pallas_call(functools.partial(filter_channels, sum(sizes[:chunk]), siz...]
    slice x2 -> x1, local copies, waits for them, and re-layouts: 2.1 us -> 1.21 us  [shards(): cur = baseband[start:start + size].reshape(4 * size, HALF, RADIX)]
  transfers between devices with their start and end apart: 3 -> 2, of which waited for: 0 -> 0; matrix products, arithmetic and copies ran while one was open for 7% -> 5% of each run, Pallas kernels for 16% -> 14%
where the time goes in v4:
time: 44 us; the launch traced here: 43.7 us
  Pallas kernels  31.7 us (72%)
  starting transfers between devices  6.5 us (15%)
  local copies, waits for them, and re-layouts  5.24 us (12%)
    pallas_call x1, Pallas kernels, shards(): pl.pallas_call(functools.partial(work_kernel, sizes, devices, factor), ou...  25.8 us
    ppermute x2, starting transfers between devices, shards(): prevs.append(lax.ppermute(cur, 'tm', route))  6.5 us
    pallas_call x1, Pallas kernels, shards(): pl.pallas_call(functools.partial(filter_channels, sum(sizes[:chunk]), siz...  3.26 us
    unnamed x20, local copies, waits for them, and re-layouts  2.7 us
    pallas_call x1, Pallas kernels, shards(): pl.pallas_call(functools.partial(prep_kernel, sizes), out_shape=[jax.Shap...  2.65 us
    slice x1, local copies, waits for them, and re-layouts, shards(): cur = baseband[start:start + size].reshape(4 * size, HALF, RADIX)  1.21 us
  transfers between devices with their start and end apart: 2, of which 0 were waited for; matrix products, arithmetic and copies ran while one was open for 5% of the time, Pallas kernels for 14%

profile of v4, /device:TPU:1, one launch (start us, length us, event | category | flops | bytes accessed | tf_op | source)
XLA Modules:
  0.0 43.7 jit_solution(4513509347091584025)
XLA Ops:
  0.0 1.2 %fusion = (bf16[4,4,8192]{2,1,0:T(4,128)(2,1)S(1)}, bf16[4,4,8192]{2,1,0:T(4,128)(2,1)S(1)}) fusion(bf16[8,4,8192]{2,1,0:T(4,128)(2,1)} %param.12), kind=kLoop, calls=%fused_computation.1 | loop fusion | bytes 1048576 | tf_op jit(solution)/shard_map/slice | solution.py:307
  1.2 0.3 reshape.12.refs_0_
  1.5 4.6 %collective-permute-start = (bf16[16,64,128]{2,1,0:T(8,128)(2,1)S(1)}, bf16[16,64,128]{2,1,0:T(8,128)(2,1)S(1)}, u32[]{:S(2)}, u32[]{:S(2)}) collective-permute-start(bf16[16,64,128]{2,1,0:T(8,128)(2,1)S(1)} %reshape.12.refs_0_), channel_id=1, source_target_pairs={{0,1},{1,2},{2,3},{3,4},{4,5},{5,6},{6,7},{7,8},{8,9},{9,10},{10,1... | collective-permute-start | bytes 786440 | tf_op jit(solution)/shard_map/ppermute | solution.py:309
  6.1 0.3 reshape.13.refs_1_
  6.4 1.9 %collective-permute-start.1 = (bf16[16,64,128]{2,1,0:T(8,128)(2,1)S(1)}, bf16[16,64,128]{2,1,0:T(8,128)(2,1)S(1)}, u32[]{:S(2)}, u32[]{:S(2)}) collective-permute-start(bf16[16,64,128]{2,1,0:T(8,128)(2,1)S(1)} %reshape.13.refs_1_), channel_id=1, source_target_pairs={{0,1},{1,2},{2,3},{3,4},{4,5},{5,6},{6,7},{7,8},{8,9},{9,10},{10,1... | collective-permute-start | bytes 786440 | tf_op jit(solution)/shard_map/ppermute | solution.py:309
  8.3 0.8 %reshape.15.refs_3_.refs_2_ = s32[32,256]{1,0:T(8,128)S(1)} reshape(s32[8192]{0:T(1024)} %param.14) | data formatting | bytes 65536 | tf_op jit(solution)/shard_map/reshape | solution.py:311
  9.1 1.1 %copy.15 = f32[1,8,128,128]{3,2,1,0:T(8,128)S(1)} copy(f32[1,8,128,128]{3,1,2,0:T(8,128)} %bitcast.5) | data formatting | bytes 1048576
  10.2 0.0 copy-start.8
  10.2 0.9 %copy-done.8 = bf16[256,256]{1,0:T(8,128)(2,1)S(1)} copy-done((bf16[256,256]{1,0:T(8,128)(2,1)S(1)}, bf16[256,256]{1,0:T(8,128)(2,1)}, u32[]{:S(2)}) %copy-start.8) | copy-done | bytes 131096
  11.1 0.0 copy-start
  11.1 0.0 copy-start.1
  11.1 0.0 copy-start.2
  11.2 0.0 copy-start.3
  11.2 0.0 copy-start.4
  11.2 0.0 copy-start.5
  11.2 0.0 copy-start.6
  11.2 0.0 copy-start.7
  11.2 2.7 %prep.1 = (f32[8,128,256]{2,1,0:T(8,128)S(1)}, f32[8,256,256]{2,1,0:T(8,128)S(1)}, bf16[256,8192]{1,0:T(8,128)(2,1)S(1)}) custom-call(bf16[16,64,128]{2,1,0:T(8,128)(2,1)S(1)} %reshape.12.refs_0_, bf16[16,64,128]{2,1,0:T(8,128)(2,1)S(1)} %reshape.13.refs_1_, f32[8,128,128]{2,1,0:T(8,128)S(1)} %bitcast.4, s32[32,256]{1,0:T(8,128)S(1)} %reshape.15.refs_3_.refs_2_, ...), custom_call_target="tpu_custom_call" | custom-call | flops 4000000000 | bytes 9437184 | tf_op jit(solution)/shard_map/prep/pallas_call | solution.py:314
  13.9 0.0 collective-permute-done.prev
  13.9 0.0 copy-done
  13.9 0.0 copy-done.1
  13.9 0.0 copy-done.2
  13.9 0.0 copy-done.3
  13.9 0.0 copy-done.4
  13.9 0.0 copy-done.5
  13.9 0.0 copy-done.6
  13.9 0.0 copy-done.7
  14.0 3.3 %filter.1.refs_0_ = f32[1024,128]{1,0:T(8,128)S(1)} custom-call(bf16[16,64,128]{2,1,0:T(8,128)(2,1)S(1)} %collective-permute-done.prev, f32[8,128,256]{2,1,0:T(8,128)S(1)} %get-tuple-element.8.gain.refs_4_, f32[8,256,256]{2,1,0:T(8,128)S(1)} %get-tuple-element.9.part.refs_5_, bf16[256,256]{1,0:T(8,128)(2,1)S(1)} %copy-done, bf16[256,256]{1,0:T(8,128)(2,1)S(1)} %copy-done.1, ...), custom_call_target="tpu_custom_call" | custom-call | flops 4000000000 | bytes 4194304 | tf_op jit(solution)/shard_map/filter/pallas_call | solution.py:333
  17.2 0.0 collective-permute-done.1.refs_3_
  17.2 25.8 %work.1 = f32[8,4,32]{2,1,0:T(4,128)S(1)} custom-call(f32[1024,128]{1,0:T(8,128)S(1)} %filter.1.refs_0_, bf16[256,8192]{1,0:T(8,128)(2,1)S(1)} %get-tuple-element.10.refs_1_, s32[32,256]{1,0:T(8,128)S(1)} %reshape.15.refs_3_.refs_2_, bf16[16,64,128]{2,1,0:T(8,128)(2,1)S(1)} %collective-permute-done.1.refs_3_, ...), custom_call_target="tpu_custom_call" | custom-call | tf_op jit(solution)/shard_map/work/pallas_call | solution.py:346
  43.0 0.6 %copy.17 = f32[8,4,32]{2,1,0:T(4,128)} copy(f32[8,4,32]{2,1,0:T(4,128)S(1)} %work.1) | data formatting | bytes 8192
Async XLA Ops:
  1.5 12.4 %collective-permute-start = (bf16[16,64,128]{2,1,0:T(8,128)(2,1)S(1)}, bf16[16,64,128]{2,1,0:T(8,128)(2,1)S(1)}, u32[]{:S(2)}, u32[]{:S(2)}) collective-permute-start(bf16[16,64,128]{2,1,0:T(8,128)(2,1)S(1)} %reshape.12.refs_0_), channel_id=1, source_target_pairs={{0,1},{1,2},{2,3},{3,4},{4,5},{5,6},{6,7},{7,8},{8,9},{9,10},{10,1... | collective-permute-start | bytes 786440 | tf_op jit(solution)/shard_map/ppermute | solution.py:309
  6.4 10.8 %collective-permute-start.1 = (bf16[16,64,128]{2,1,0:T(8,128)(2,1)S(1)}, bf16[16,64,128]{2,1,0:T(8,128)(2,1)S(1)}, u32[]{:S(2)}, u32[]{:S(2)}) collective-permute-start(bf16[16,64,128]{2,1,0:T(8,128)(2,1)S(1)} %reshape.13.refs_1_), channel_id=1, source_target_pairs={{0,1},{1,2},{2,3},{3,4},{4,5},{5,6},{6,7},{7,8},{8,9},{9,10},{10,1... | collective-permute-start | bytes 786440 | tf_op jit(solution)/shard_map/ppermute | solution.py:309
  10.2 0.9 %copy-start.8 = (bf16[256,256]{1,0:T(8,128)(2,1)S(1)}, bf16[256,256]{1,0:T(8,128)(2,1)}, u32[]{:S(2)}) copy-start(bf16[256,256]{1,0:T(8,128)(2,1)} %constant.18.clone.refs_4_) | copy-start | bytes 393220
  11.1 2.7 %copy-start = (bf16[256,256]{1,0:T(8,128)(2,1)S(1)}, bf16[256,256]{1,0:T(8,128)(2,1)}, u32[]{:S(2)}) copy-start(bf16[256,256]{1,0:T(8,128)(2,1)} %constant.19.clone.left.refs_6_) | copy-start | bytes 393220
  11.1 2.7 %copy-start.1 = (bf16[256,256]{1,0:T(8,128)(2,1)S(1)}, bf16[256,256]{1,0:T(8,128)(2,1)}, u32[]{:S(2)}) copy-start(bf16[256,256]{1,0:T(8,128)(2,1)} %constant.20.clone.right_h.refs_7_) | copy-start | bytes 393220
  11.1 2.7 %copy-start.2 = (bf16[256,256]{1,0:T(8,128)(2,1)S(1)}, bf16[256,256]{1,0:T(8,128)(2,1)}, u32[]{:S(2)}) copy-start(bf16[256,256]{1,0:T(8,128)(2,1)} %constant.21.clone.right_l.refs_8_) | copy-start | bytes 393220
  11.2 2.8 %copy-start.3 = (bf16[256,256]{1,0:T(8,128)(2,1)S(1)}, bf16[256,256]{1,0:T(8,128)(2,1)}, u32[]{:S(2)}) copy-start(bf16[256,256]{1,0:T(8,128)(2,1)} %constant.22.clone.back_right_h.refs_9_) | copy-start | bytes 393220
  11.2 2.8 %copy-start.4 = (bf16[256,256]{1,0:T(8,128)(2,1)S(1)}, bf16[256,256]{1,0:T(8,128)(2,1)}, u32[]{:S(2)}) copy-start(bf16[256,256]{1,0:T(8,128)(2,1)} %constant.23.clone.back_right_l.refs_10_) | copy-start | bytes 393220
  11.2 2.8 %copy-start.5 = (f32[128,256]{1,0:T(8,128)S(1)}, f32[128,256]{1,0:T(8,128)}, u32[]{:S(2)}) copy-start(f32[128,256]{1,0:T(8,128)} %constant.26.clone.twist.refs_13_) | copy-start | bytes 393220
  11.2 2.8 %copy-start.6 = (bf16[128,256]{1,0:T(8,128)(2,1)S(1)}, bf16[128,256]{1,0:T(8,128)(2,1)}, u32[]{:S(2)}) copy-start(bf16[128,256]{1,0:T(8,128)(2,1)} %constant.24.clone.back_left_h.refs_11_) | copy-start | bytes 196612
  11.2 2.8 %copy-start.7 = (bf16[128,256]{1,0:T(8,128)(2,1)S(1)}, bf16[128,256]{1,0:T(8,128)(2,1)}, u32[]{:S(2)}) copy-start(bf16[128,256]{1,0:T(8,128)(2,1)} %constant.25.clone.back_left_l.refs_12_) | copy-start | bytes 196612

commit v5 on v4

--- a/solution.py
+++ b/solution.py
@@ -37,8 +37,9 @@
     for part in range(2):
         columns = np.arange(4 * HALF).reshape(4, HALF)[part::2].reshape(-1)
         tables.append(np.concatenate(split_table(left[:, columns]), axis=1))
-    for table in (right, back_right, back_left):
+    for table in (right, back_right):
         tables.extend(split_table(table))
+    tables.append(np.concatenate(split_table(back_left), axis=0))
     return tables, twist
 
 
@@ -103,7 +104,7 @@
 
 def filter_channels(
     start, size, prev, gain, part, left, right_h, right_l, back_right_h, back_right_l,
-    back_left_h, back_left_l, twist, stokes,
+    back_left, twist, stokes,
 ):
     rows = 4 * size
     twist_real = twist[:, :RADIX]
@@ -111,46 +112,57 @@
     wide_real = jnp.concatenate([twist_real, twist_real], axis=1)
     wide_imag = jnp.concatenate([twist_imag, twist_imag], axis=1)
 
+    def twice(value):
+        return jnp.concatenate([value, value], axis=0)
+
+    tall_real, tall_imag = twice(twist_real), twice(twist_imag)
+
     def channel(c):
         base = 4 * c
         section = part[start + c] + first_stage(left, prev, base)
         real, imag = section[:RADIX], section[RADIX:]
         turned_real = real * wide_real - imag * wide_imag
         turned_imag = real * wide_imag + imag * wide_real
-        gain_real, gain_imag = gain[start + c, :, :RADIX], gain[start + c, :, RADIX:]
-        waves_real, waves_imag = [], []
-        for p in range(2):
-            lanes = slice(p * RADIX, (p + 1) * RADIX)
-            high, low = halves(
-                jnp.concatenate([turned_real[:, lanes], turned_imag[:, lanes]], axis=1)
-            )
-            spec = dot(high, right_h[...]) + dot(low, right_h[...]) + dot(high, right_l[...])
-            spec_real, spec_imag = spec[:, :RADIX], spec[:, RADIX:]
-            high, low = halves(
-                jnp.concatenate(
-                    [
-                        spec_real * gain_real - spec_imag * gain_imag,
-                        spec_real * gain_imag + spec_imag * gain_real,
-                    ],
-                    axis=1,
-                )
-            )
-            back = (
-                dot(high, back_right_h[...])
-                + dot(low, back_right_h[...])
-                + dot(high, back_right_l[...])
-            )
-            back_real, back_imag = back[:, :RADIX], back[:, RADIX:]
-            waves_real.append(back_real * twist_real + back_imag * twist_imag)
-            waves_imag.append(back_imag * twist_real - back_real * twist_imag)
+        gain_real, gain_imag = twice(gain[start + c, :, :RADIX]), twice(gain[start + c, :, RADIX:])
         high, low = halves(
             jnp.concatenate(
-                [jnp.concatenate(waves_real, axis=1), jnp.concatenate(waves_imag, axis=1)], axis=0
+                [
+                    jnp.concatenate([turned_real[:, :RADIX], turned_imag[:, :RADIX]], axis=1),
+                    jnp.concatenate([turned_real[:, RADIX:], turned_imag[:, RADIX:]], axis=1),
+                ],
+                axis=0,
             )
         )
-        wave = (
-            dot(back_left_h[...], high) + dot(back_left_h[...], low) + dot(back_left_l[...], high)
-        )
+        spec = dot(high, right_h[...]) + dot(low, right_h[...]) + dot(high, right_l[...])
+        spec_real, spec_imag = spec[:, :RADIX], spec[:, RADIX:]
+        high, low = halves(
+            jnp.concatenate(
+                [
+                    spec_real * gain_real - spec_imag * gain_imag,
+                    spec_real * gain_imag + spec_imag * gain_real,
+                ],
+                axis=1,
+            )
+        )
+        back = (
+            dot(high, back_right_h[...])
+            + dot(low, back_right_h[...])
+            + dot(high, back_right_l[...])
+        )
+        back_real, back_imag = back[:, :RADIX], back[:, RADIX:]
+        wave_real = back_real * tall_real + back_imag * tall_imag
+        wave_imag = back_imag * tall_real - back_real * tall_imag
+        high, low = halves(
+            jnp.concatenate(
+                [
+                    jnp.concatenate([wave_real[:RADIX], wave_imag[:RADIX]], axis=0),
+                    jnp.concatenate([wave_real[RADIX:], wave_imag[RADIX:]], axis=0),
+                ],
+                axis=1,
+            )
+        )
+        both = dot(back_left[...], high)
+        wave = both[:RADIX] + both[RADIX:] + dot(back_left[:RADIX, :], low)
         xr, xi = wave[:HALF, :RADIX], wave[HALF:, :RADIX]
         yr, yi = wave[:HALF, RADIX:], wave[HALF:, RADIX:]
         first = xr * xr + xi * xi
@@ -170,8 +182,8 @@
 
 def work_kernel(sizes, devices, factor, *refs):
     ready, refs = refs[:len(sizes) - 1], refs[len(sizes) - 1:]
-    onehot, bins, *operands = refs[:13]
-    out, last, picked, tiles, swapped, sums, landed, *sems = refs[13:]
+    onehot, bins, *operands = refs[:12]
+    out, last, picked, tiles, swapped, sums, landed, *sems = refs[12:]
     swap_sems, send_sems, recv_sems = sems
     me = lax.axis_index("tm")
     barrier = pltpu.get_barrier_semaphore()
@@ -333,7 +345,7 @@
             pl.pallas_call(
                 functools.partial(filter_channels, sum(sizes[:chunk]), size),
                 out_shape=jax.ShapeDtypeStruct((HALF * 4 * size, RADIX), F32),
-                in_specs=[in_vmem] * 11,
+                in_specs=[in_vmem] * 10,
                 out_specs=in_vmem,
                 compiler_params=pltpu.CompilerParams(vmem_limit_bytes=24 * 2**20),
                 cost_estimate=pl.CostEstimate(
@@ -346,7 +358,7 @@
     return pl.pallas_call(
         functools.partial(work_kernel, sizes, devices, factor),
         out_shape=jax.ShapeDtypeStruct((channels, 4, BINS // devices), F32),
-        in_specs=[in_vmem] * (len(ready) + 13),
+        in_specs=[in_vmem] * (len(ready) + 12),
         out_specs=in_vmem,
         scratch_shapes=[
             pltpu.VMEM((HALF * 4 * sizes[-1], RADIX), F32),

time: 44 us -> 44 us (level)
    unnamed x20 -> x18, local copies, waits for them, and re-layouts: 2.7 us -> 2.69 us
where the time goes in v5:
time: 44 us; the launch traced here: 43.7 us
  Pallas kernels  31.8 us (72%)
  starting transfers between devices  6.5 us (15%)
  local copies, waits for them, and re-layouts  5.23 us (12%)
    pallas_call x1, Pallas kernels, shards(): pl.pallas_call(functools.partial(work_kernel, sizes, devices, factor), ou...  25.6 us
    ppermute x2, starting transfers between devices, shards(): prevs.append(lax.ppermute(cur, 'tm', route))  6.5 us
    pallas_call x1, Pallas kernels, shards(): pl.pallas_call(functools.partial(filter_channels, sum(sizes[:chunk]), siz...  3.52 us
    unnamed x18, local copies, waits for them, and re-layouts  2.69 us
    pallas_call x1, Pallas kernels, shards(): pl.pallas_call(functools.partial(prep_kernel, sizes), out_shape=[jax.Shap...  2.65 us
    slice x1, local copies, waits for them, and re-layouts, shards(): cur = baseband[start:start + size].reshape(4 * size, HALF, RADIX)  1.21 us
  transfers between devices with their start and end apart: 2, of which 0 were waited for; matrix products, arithmetic and copies ran while one was open for 5% of the time, Pallas kernels for 14%

profile of v5, /device:TPU:1, one launch (start us, length us, event | category | flops | bytes accessed | tf_op | source)
XLA Modules:
  0.0 43.7 jit_solution(6057555020959627384)
XLA Ops:
  0.0 1.2 %fusion = (bf16[4,4,8192]{2,1,0:T(4,128)(2,1)S(1)}, bf16[4,4,8192]{2,1,0:T(4,128)(2,1)S(1)}) fusion(bf16[8,4,8192]{2,1,0:T(4,128)(2,1)} %param.11), kind=kLoop, calls=%fused_computation.1 | loop fusion | bytes 1048576 | tf_op jit(solution)/shard_map/slice | solution.py:319
  1.2 0.3 reshape.12.refs_0_
  1.5 4.6 %collective-permute-start = (bf16[16,64,128]{2,1,0:T(8,128)(2,1)S(1)}, bf16[16,64,128]{2,1,0:T(8,128)(2,1)S(1)}, u32[]{:S(2)}, u32[]{:S(2)}) collective-permute-start(bf16[16,64,128]{2,1,0:T(8,128)(2,1)S(1)} %reshape.12.refs_0_), channel_id=1, source_target_pairs={{0,1},{1,2},{2,3},{3,4},{4,5},{5,6},{6,7},{7,8},{8,9},{9,10},{10,1... | collective-permute-start | bytes 786440 | tf_op jit(solution)/shard_map/ppermute | solution.py:321
  6.1 0.3 reshape.13.refs_1_
  6.4 1.9 %collective-permute-start.1 = (bf16[16,64,128]{2,1,0:T(8,128)(2,1)S(1)}, bf16[16,64,128]{2,1,0:T(8,128)(2,1)S(1)}, u32[]{:S(2)}, u32[]{:S(2)}) collective-permute-start(bf16[16,64,128]{2,1,0:T(8,128)(2,1)S(1)} %reshape.13.refs_1_), channel_id=1, source_target_pairs={{0,1},{1,2},{2,3},{3,4},{4,5},{5,6},{6,7},{7,8},{8,9},{9,10},{10,1... | collective-permute-start | bytes 786440 | tf_op jit(solution)/shard_map/ppermute | solution.py:321
  8.3 0.8 %reshape.15.refs_3_.refs_2_ = s32[32,256]{1,0:T(8,128)S(1)} reshape(s32[8192]{0:T(1024)} %param.13) | data formatting | bytes 65536 | tf_op jit(solution)/shard_map/reshape | solution.py:323
  9.1 1.1 %copy.14 = f32[1,8,128,128]{3,2,1,0:T(8,128)S(1)} copy(f32[1,8,128,128]{3,1,2,0:T(8,128)} %bitcast.5) | data formatting | bytes 1048576
  10.2 0.0 copy-start.7
  10.2 0.9 %copy-done.7 = bf16[256,256]{1,0:T(8,128)(2,1)S(1)} copy-done((bf16[256,256]{1,0:T(8,128)(2,1)S(1)}, bf16[256,256]{1,0:T(8,128)(2,1)}, u32[]{:S(2)}) %copy-start.7) | copy-done | bytes 131096
  11.1 0.0 copy-start
  11.1 0.0 copy-start.1
  11.1 0.0 copy-start.2
  11.2 0.0 copy-start.3
  11.2 0.0 copy-start.4
  11.2 0.0 copy-start.5
  11.2 0.0 copy-start.6
  11.2 2.6 %prep.1 = (f32[8,128,256]{2,1,0:T(8,128)S(1)}, f32[8,256,256]{2,1,0:T(8,128)S(1)}, bf16[256,8192]{1,0:T(8,128)(2,1)S(1)}) custom-call(bf16[16,64,128]{2,1,0:T(8,128)(2,1)S(1)} %reshape.12.refs_0_, bf16[16,64,128]{2,1,0:T(8,128)(2,1)S(1)} %reshape.13.refs_1_, f32[8,128,128]{2,1,0:T(8,128)S(1)} %bitcast.4, s32[32,256]{1,0:T(8,128)S(1)} %reshape.15.refs_3_.refs_2_, ...), custom_call_target="tpu_custom_call" | custom-call | flops 4000000000 | bytes 9437184 | tf_op jit(solution)/shard_map/prep/pallas_call | solution.py:326
  13.8 0.0 collective-permute-done.prev
  13.9 0.0 copy-done
  13.9 0.0 copy-done.1
  13.9 0.0 copy-done.2
  13.9 0.0 copy-done.3
  13.9 0.0 copy-done.4
  13.9 0.0 copy-done.5
  13.9 0.0 copy-done.6
  13.9 3.5 %filter.1.refs_0_ = f32[1024,128]{1,0:T(8,128)S(1)} custom-call(bf16[16,64,128]{2,1,0:T(8,128)(2,1)S(1)} %collective-permute-done.prev, f32[8,128,256]{2,1,0:T(8,128)S(1)} %get-tuple-element.8.gain.refs_4_, f32[8,256,256]{2,1,0:T(8,128)S(1)} %get-tuple-element.9.part.refs_5_, bf16[256,256]{1,0:T(8,128)(2,1)S(1)} %copy-done, bf16[256,256]{1,0:T(8,128)(2,1)S(1)} %copy-done.1, ...), custom_call_target="tpu_custom_call" | custom-call | flops 4000000000 | bytes 4194304 | tf_op jit(solution)/shard_map/filter/pallas_call | solution.py:345
  17.5 0.0 collective-permute-done.1.refs_3_
  17.5 25.6 %work.1 = f32[8,4,32]{2,1,0:T(4,128)S(1)} custom-call(f32[1024,128]{1,0:T(8,128)S(1)} %filter.1.refs_0_, bf16[256,8192]{1,0:T(8,128)(2,1)S(1)} %get-tuple-element.10.refs_1_, s32[32,256]{1,0:T(8,128)S(1)} %reshape.15.refs_3_.refs_2_, bf16[16,64,128]{2,1,0:T(8,128)(2,1)S(1)} %collective-permute-done.1.refs_3_, ...), custom_call_target="tpu_custom_call" | custom-call | tf_op jit(solution)/shard_map/work/pallas_call | solution.py:358
  43.1 0.6 %copy.16 = f32[8,4,32]{2,1,0:T(4,128)} copy(f32[8,4,32]{2,1,0:T(4,128)S(1)} %work.1) | data formatting | bytes 8192
Async XLA Ops:
  1.5 12.3 %collective-permute-start = (bf16[16,64,128]{2,1,0:T(8,128)(2,1)S(1)}, bf16[16,64,128]{2,1,0:T(8,128)(2,1)S(1)}, u32[]{:S(2)}, u32[]{:S(2)}) collective-permute-start(bf16[16,64,128]{2,1,0:T(8,128)(2,1)S(1)} %reshape.12.refs_0_), channel_id=1, source_target_pairs={{0,1},{1,2},{2,3},{3,4},{4,5},{5,6},{6,7},{7,8},{8,9},{9,10},{10,1... | collective-permute-start | bytes 786440 | tf_op jit(solution)/shard_map/ppermute | solution.py:321
  6.4 11.1 %collective-permute-start.1 = (bf16[16,64,128]{2,1,0:T(8,128)(2,1)S(1)}, bf16[16,64,128]{2,1,0:T(8,128)(2,1)S(1)}, u32[]{:S(2)}, u32[]{:S(2)}) collective-permute-start(bf16[16,64,128]{2,1,0:T(8,128)(2,1)S(1)} %reshape.13.refs_1_), channel_id=1, source_target_pairs={{0,1},{1,2},{2,3},{3,4},{4,5},{5,6},{6,7},{7,8},{8,9},{9,10},{10,1... | collective-permute-start | bytes 786440 | tf_op jit(solution)/shard_map/ppermute | solution.py:321
  10.2 0.9 %copy-start.7 = (bf16[256,256]{1,0:T(8,128)(2,1)S(1)}, bf16[256,256]{1,0:T(8,128)(2,1)}, u32[]{:S(2)}) copy-start(bf16[256,256]{1,0:T(8,128)(2,1)} %constant.16.clone.refs_4_) | copy-start | bytes 393220
  11.1 2.7 %copy-start = (bf16[256,256]{1,0:T(8,128)(2,1)S(1)}, bf16[256,256]{1,0:T(8,128)(2,1)}, u32[]{:S(2)}) copy-start(bf16[256,256]{1,0:T(8,128)(2,1)} %constant.17.clone.left.refs_6_) | copy-start | bytes 393220
  11.1 2.7 %copy-start.1 = (bf16[256,256]{1,0:T(8,128)(2,1)S(1)}, bf16[256,256]{1,0:T(8,128)(2,1)}, u32[]{:S(2)}) copy-start(bf16[256,256]{1,0:T(8,128)(2,1)} %constant.18.clone.right_h.refs_7_) | copy-start | bytes 393220
  11.1 2.7 %copy-start.2 = (bf16[256,256]{1,0:T(8,128)(2,1)S(1)}, bf16[256,256]{1,0:T(8,128)(2,1)}, u32[]{:S(2)}) copy-start(bf16[256,256]{1,0:T(8,128)(2,1)} %constant.19.clone.right_l.refs_8_) | copy-start | bytes 393220
  11.2 2.7 %copy-start.3 = (bf16[256,256]{1,0:T(8,128)(2,1)S(1)}, bf16[256,256]{1,0:T(8,128)(2,1)}, u32[]{:S(2)}) copy-start(bf16[256,256]{1,0:T(8,128)(2,1)} %constant.20.clone.back_right_h.refs_9_) | copy-start | bytes 393220
  11.2 2.7 %copy-start.4 = (bf16[256,256]{1,0:T(8,128)(2,1)S(1)}, bf16[256,256]{1,0:T(8,128)(2,1)}, u32[]{:S(2)}) copy-start(bf16[256,256]{1,0:T(8,128)(2,1)} %constant.21.clone.back_right_l.refs_10_) | copy-start | bytes 393220
  11.2 2.7 %copy-start.5 = (bf16[256,256]{1,0:T(8,128)(2,1)S(1)}, bf16[256,256]{1,0:T(8,128)(2,1)}, u32[]{:S(2)}) copy-start(bf16[256,256]{1,0:T(8,128)(2,1)} %constant.22.clone.back_left.refs_11_) | copy-start | bytes 393220
  11.2 2.7 %copy-start.6 = (f32[128,256]{1,0:T(8,128)S(1)}, f32[128,256]{1,0:T(8,128)}, u32[]{:S(2)}) copy-start(f32[128,256]{1,0:T(8,128)} %constant.23.clone.twist.refs_12_) | copy-start | bytes 393220

commit v6 on v4

--- a/solution.py
+++ b/solution.py
@@ -160,12 +160,12 @@
         stokes[pl.ds(base + 2, HALF, rows), :] = 2.0 * (xr * yr + xi * yi)
         stokes[pl.ds(base + 3, HALF, rows), :] = 2.0 * (xr * yi - xi * yr)
 
-    def channel_pair(i, carry):
-        channel(2 * i)
-        channel(2 * i + 1)
-        return carry
-
-    lax.fori_loop(0, size // 2, channel_pair, 0)
+    def channel_group(i, carry):
+        for step in range(4):
+            channel(4 * i + step)
+        return carry
+
+    lax.fori_loop(0, size // 4, channel_group, 0)
 
 
 def work_kernel(sizes, devices, factor, *refs):
@@ -227,7 +227,7 @@
             ).astype(BF16)
         return carry
 
-    lax.fori_loop(0, HALF // 2, pick, 0, unroll=4)
+    lax.fori_loop(0, HALF // 2, pick, 0, unroll=8)
 
     total = lax.dot_general(
         picked[...], onehot[...], (((1,), (1,)), ((), ())), preferred_element_type=F32

time: 44 us -> 44.2 us (level)
    pallas_call x1, Pallas kernels: 25.8 us -> 26.5 us  [shards(): pl.pallas_call(functools.partial(work_kernel, sizes, devices, factor), ou...]
    pallas_call x1, Pallas kernels: 3.26 us -> 2.79 us  [shards(): pl.pallas_call(functools.partial(filter_channels, sum(sizes[:chunk]), siz...]
  transfers between devices with their start and end apart: 2 -> 2, of which waited for: 0 -> 0; matrix products, arithmetic and copies ran while one was open for 5% -> 5% of each run, Pallas kernels for 14% -> 12%
where the time goes in v6:
time: 44.2 us; the launch traced here: 43.9 us
  Pallas kernels  32 us (72%)
  starting transfers between devices  6.5 us (15%)
  local copies, waits for them, and re-layouts  5.24 us (12%)
    pallas_call x1, Pallas kernels, shards(): pl.pallas_call(functools.partial(work_kernel, sizes, devices, factor), ou...  26.5 us
    ppermute x2, starting transfers between devices, shards(): prevs.append(lax.ppermute(cur, 'tm', route))  6.5 us
    pallas_call x1, Pallas kernels, shards(): pl.pallas_call(functools.partial(filter_channels, sum(sizes[:chunk]), siz...  2.79 us
    unnamed x20, local copies, waits for them, and re-layouts  2.7 us
    pallas_call x1, Pallas kernels, shards(): pl.pallas_call(functools.partial(prep_kernel, sizes), out_shape=[jax.Shap...  2.65 us
    slice x1, local copies, waits for them, and re-layouts, shards(): cur = baseband[start:start + size].reshape(4 * size, HALF, RADIX)  1.21 us
  transfers between devices with their start and end apart: 2, of which 0 were waited for; matrix products, arithmetic and copies ran while one was open for 5% of the time, Pallas kernels for 12%

profile of v6, /device:TPU:1, one launch (start us, length us, event | category | flops | bytes accessed | tf_op | source)
XLA Modules:
  0.0 43.9 jit_solution(16193009143983272850)
XLA Ops:
  0.0 1.2 %fusion = (bf16[4,4,8192]{2,1,0:T(4,128)(2,1)S(1)}, bf16[4,4,8192]{2,1,0:T(4,128)(2,1)S(1)}) fusion(bf16[8,4,8192]{2,1,0:T(4,128)(2,1)} %param.12), kind=kLoop, calls=%fused_computation.1 | loop fusion | bytes 1048576 | tf_op jit(solution)/shard_map/slice | solution.py:307
  1.2 0.3 reshape.12.refs_0_
  1.5 4.6 %collective-permute-start = (bf16[16,64,128]{2,1,0:T(8,128)(2,1)S(1)}, bf16[16,64,128]{2,1,0:T(8,128)(2,1)S(1)}, u32[]{:S(2)}, u32[]{:S(2)}) collective-permute-start(bf16[16,64,128]{2,1,0:T(8,128)(2,1)S(1)} %reshape.12.refs_0_), channel_id=1, source_target_pairs={{0,1},{1,2},{2,3},{3,4},{4,5},{5,6},{6,7},{7,8},{8,9},{9,10},{10,1... | collective-permute-start | bytes 786440 | tf_op jit(solution)/shard_map/ppermute | solution.py:309
  6.1 0.3 reshape.13.refs_1_
  6.4 1.9 %collective-permute-start.1 = (bf16[16,64,128]{2,1,0:T(8,128)(2,1)S(1)}, bf16[16,64,128]{2,1,0:T(8,128)(2,1)S(1)}, u32[]{:S(2)}, u32[]{:S(2)}) collective-permute-start(bf16[16,64,128]{2,1,0:T(8,128)(2,1)S(1)} %reshape.13.refs_1_), channel_id=1, source_target_pairs={{0,1},{1,2},{2,3},{3,4},{4,5},{5,6},{6,7},{7,8},{8,9},{9,10},{10,1... | collective-permute-start | bytes 786440 | tf_op jit(solution)/shard_map/ppermute | solution.py:309
  8.3 0.8 %reshape.15.refs_3_.refs_2_ = s32[32,256]{1,0:T(8,128)S(1)} reshape(s32[8192]{0:T(1024)} %param.14) | data formatting | bytes 65536 | tf_op jit(solution)/shard_map/reshape | solution.py:311
  9.1 1.1 %copy.15 = f32[1,8,128,128]{3,2,1,0:T(8,128)S(1)} copy(f32[1,8,128,128]{3,1,2,0:T(8,128)} %bitcast.5) | data formatting | bytes 1048576
  10.2 0.0 copy-start.8
  10.2 0.9 %copy-done.8 = bf16[256,256]{1,0:T(8,128)(2,1)S(1)} copy-done((bf16[256,256]{1,0:T(8,128)(2,1)S(1)}, bf16[256,256]{1,0:T(8,128)(2,1)}, u32[]{:S(2)}) %copy-start.8) | copy-done | bytes 131096
  11.1 0.0 copy-start
  11.1 0.0 copy-start.1
  11.1 0.0 copy-start.2
  11.2 0.0 copy-start.3
  11.2 0.0 copy-start.4
  11.2 0.0 copy-start.5
  11.2 0.0 copy-start.6
  11.2 0.0 copy-start.7
  11.2 2.7 %prep.1 = (f32[8,128,256]{2,1,0:T(8,128)S(1)}, f32[8,256,256]{2,1,0:T(8,128)S(1)}, bf16[256,8192]{1,0:T(8,128)(2,1)S(1)}) custom-call(bf16[16,64,128]{2,1,0:T(8,128)(2,1)S(1)} %reshape.12.refs_0_, bf16[16,64,128]{2,1,0:T(8,128)(2,1)S(1)} %reshape.13.refs_1_, f32[8,128,128]{2,1,0:T(8,128)S(1)} %bitcast.4, s32[32,256]{1,0:T(8,128)S(1)} %reshape.15.refs_3_.refs_2_, ...), custom_call_target="tpu_custom_call" | custom-call | flops 4000000000 | bytes 9437184 | tf_op jit(solution)/shard_map/prep/pallas_call | solution.py:314
  13.9 0.0 collective-permute-done.prev
  13.9 0.0 copy-done
  13.9 0.0 copy-done.1
  13.9 0.0 copy-done.2
  13.9 0.0 copy-done.3
  13.9 0.0 copy-done.4
  13.9 0.0 copy-done.5
  13.9 0.0 copy-done.6
  13.9 0.0 copy-done.7
  14.0 2.8 %filter.1.refs_0_ = f32[1024,128]{1,0:T(8,128)S(1)} custom-call(bf16[16,64,128]{2,1,0:T(8,128)(2,1)S(1)} %collective-permute-done.prev, f32[8,128,256]{2,1,0:T(8,128)S(1)} %get-tuple-element.8.gain.refs_4_, f32[8,256,256]{2,1,0:T(8,128)S(1)} %get-tuple-element.9.part.refs_5_, bf16[256,256]{1,0:T(8,128)(2,1)S(1)} %copy-done, bf16[256,256]{1,0:T(8,128)(2,1)S(1)} %copy-done.1, ...), custom_call_target="tpu_custom_call" | custom-call | flops 4000000000 | bytes 4194304 | tf_op jit(solution)/shard_map/filter/pallas_call | solution.py:333
  16.8 0.0 collective-permute-done.1.refs_3_
  16.8 26.5 %work.1 = f32[8,4,32]{2,1,0:T(4,128)S(1)} custom-call(f32[1024,128]{1,0:T(8,128)S(1)} %filter.1.refs_0_, bf16[256,8192]{1,0:T(8,128)(2,1)S(1)} %get-tuple-element.10.refs_1_, s32[32,256]{1,0:T(8,128)S(1)} %reshape.15.refs_3_.refs_2_, bf16[16,64,128]{2,1,0:T(8,128)(2,1)S(1)} %collective-permute-done.1.refs_3_, ...), custom_call_target="tpu_custom_call" | custom-call | tf_op jit(solution)/shard_map/work/pallas_call | solution.py:346
  43.3 0.6 %copy.17 = f32[8,4,32]{2,1,0:T(4,128)} copy(f32[8,4,32]{2,1,0:T(4,128)S(1)} %work.1) | data formatting | bytes 8192
Async XLA Ops:
  1.5 12.4 %collective-permute-start = (bf16[16,64,128]{2,1,0:T(8,128)(2,1)S(1)}, bf16[16,64,128]{2,1,0:T(8,128)(2,1)S(1)}, u32[]{:S(2)}, u32[]{:S(2)}) collective-permute-start(bf16[16,64,128]{2,1,0:T(8,128)(2,1)S(1)} %reshape.12.refs_0_), channel_id=1, source_target_pairs={{0,1},{1,2},{2,3},{3,4},{4,5},{5,6},{6,7},{7,8},{8,9},{9,10},{10,1... | collective-permute-start | bytes 786440 | tf_op jit(solution)/shard_map/ppermute | solution.py:309
  6.4 10.4 %collective-permute-start.1 = (bf16[16,64,128]{2,1,0:T(8,128)(2,1)S(1)}, bf16[16,64,128]{2,1,0:T(8,128)(2,1)S(1)}, u32[]{:S(2)}, u32[]{:S(2)}) collective-permute-start(bf16[16,64,128]{2,1,0:T(8,128)(2,1)S(1)} %reshape.13.refs_1_), channel_id=1, source_target_pairs={{0,1},{1,2},{2,3},{3,4},{4,5},{5,6},{6,7},{7,8},{8,9},{9,10},{10,1... | collective-permute-start | bytes 786440 | tf_op jit(solution)/shard_map/ppermute | solution.py:309
  10.2 0.9 %copy-start.8 = (bf16[256,256]{1,0:T(8,128)(2,1)S(1)}, bf16[256,256]{1,0:T(8,128)(2,1)}, u32[]{:S(2)}) copy-start(bf16[256,256]{1,0:T(8,128)(2,1)} %constant.18.clone.refs_4_) | copy-start | bytes 393220
  11.1 2.7 %copy-start = (bf16[256,256]{1,0:T(8,128)(2,1)S(1)}, bf16[256,256]{1,0:T(8,128)(2,1)}, u32[]{:S(2)}) copy-start(bf16[256,256]{1,0:T(8,128)(2,1)} %constant.19.clone.left.refs_6_) | copy-start | bytes 393220
  11.1 2.7 %copy-start.1 = (bf16[256,256]{1,0:T(8,128)(2,1)S(1)}, bf16[256,256]{1,0:T(8,128)(2,1)}, u32[]{:S(2)}) copy-start(bf16[256,256]{1,0:T(8,128)(2,1)} %constant.20.clone.right_h.refs_7_) | copy-start | bytes 393220
  11.1 2.7 %copy-start.2 = (bf16[256,256]{1,0:T(8,128)(2,1)S(1)}, bf16[256,256]{1,0:T(8,128)(2,1)}, u32[]{:S(2)}) copy-start(bf16[256,256]{1,0:T(8,128)(2,1)} %constant.21.clone.right_l.refs_8_) | copy-start | bytes 393220
  11.2 2.8 %copy-start.3 = (bf16[256,256]{1,0:T(8,128)(2,1)S(1)}, bf16[256,256]{1,0:T(8,128)(2,1)}, u32[]{:S(2)}) copy-start(bf16[256,256]{1,0:T(8,128)(2,1)} %constant.22.clone.back_right_h.refs_9_) | copy-start | bytes 393220
  11.2 2.8 %copy-start.4 = (bf16[256,256]{1,0:T(8,128)(2,1)S(1)}, bf16[256,256]{1,0:T(8,128)(2,1)}, u32[]{:S(2)}) copy-start(bf16[256,256]{1,0:T(8,128)(2,1)} %constant.23.clone.back_right_l.refs_10_) | copy-start | bytes 393220
  11.2 2.8 %copy-start.5 = (f32[128,256]{1,0:T(8,128)S(1)}, f32[128,256]{1,0:T(8,128)}, u32[]{:S(2)}) copy-start(f32[128,256]{1,0:T(8,128)} %constant.26.clone.twist.refs_13_) | copy-start | bytes 393220
  11.2 2.8 %copy-start.6 = (bf16[128,256]{1,0:T(8,128)(2,1)S(1)}, bf16[128,256]{1,0:T(8,128)(2,1)}, u32[]{:S(2)}) copy-start(bf16[128,256]{1,0:T(8,128)(2,1)} %constant.24.clone.back_left_h.refs_11_) | copy-start | bytes 196612
  11.2 2.8 %copy-start.7 = (bf16[128,256]{1,0:T(8,128)(2,1)S(1)}, bf16[128,256]{1,0:T(8,128)(2,1)}, u32[]{:S(2)}) copy-start(bf16[128,256]{1,0:T(8,128)(2,1)} %constant.25.clone.back_left_l.refs_12_) | copy-start | bytes 196612

commit v7 on v4

--- a/solution.py
+++ b/solution.py
@@ -306,6 +306,7 @@
         start = sum(sizes[:chunk])
         cur = baseband[start:start + size].reshape(4 * size, HALF, RADIX)
         curs.append(cur)
+        cur, baseband = lax.optimization_barrier((cur, baseband))
         prevs.append(lax.ppermute(cur, "tm", route))
     chirp = chirp_phase.reshape(channels, RADIX, RADIX)
     bins = phase_bins.reshape(samples // (2 * RADIX), 2 * RADIX)

time: 44 us -> 43.9 us (level)
  Pallas kernels: 31.7 us -> 30.7 us
  local copies, waits for them, and re-layouts: 5.24 us -> 6.12 us
    pallas_call x1, Pallas kernels: 25.8 us -> 24.8 us  [shards(): pl.pallas_call(functools.partial(work_kernel, sizes, devices, factor), ou...]
    slice x1 -> x2, local copies, waits for them, and re-layouts: 1.21 us -> 2.09 us  [shards(): cur = baseband[start:start + size].reshape(4 * size, HALF, RADIX)]
  transfers between devices with their start and end apart: 2 -> 2, of which waited for: 0 -> 0; matrix products, arithmetic and copies ran while one was open for 5% -> 7% of each run, Pallas kernels for 14% -> 14%
where the time goes in v7:
time: 43.9 us; the launch traced here: 43.6 us
  Pallas kernels  30.7 us (70%)
  starting transfers between devices  6.5 us (15%)
  local copies, waits for them, and re-layouts  6.12 us (14%)
    pallas_call x1, Pallas kernels, shards(): pl.pallas_call(functools.partial(work_kernel, sizes, devices, factor), ou...  24.8 us
    ppermute x2, starting transfers between devices, shards(): prevs.append(lax.ppermute(cur, 'tm', route))  6.5 us
    pallas_call x1, Pallas kernels, shards(): pl.pallas_call(functools.partial(filter_channels, sum(sizes[:chunk]), siz...  3.27 us
    unnamed x20, local copies, waits for them, and re-layouts  2.7 us
    pallas_call x1, Pallas kernels, shards(): pl.pallas_call(functools.partial(prep_kernel, sizes), out_shape=[jax.Shap...  2.64 us
    slice x2, local copies, waits for them, and re-layouts, shards(): cur = baseband[start:start + size].reshape(4 * size, HALF, RADIX)  2.09 us
  transfers between devices with their start and end apart: 2, of which 0 were waited for; matrix products, arithmetic and copies ran while one was open for 7% of the time, Pallas kernels for 14%

profile of v7, /device:TPU:1, one launch (start us, length us, event | category | flops | bytes accessed | tf_op | source)
XLA Modules:
  0.0 43.6 jit_solution(9791370722036114880)
XLA Ops:
  0.0 1.0 %slice.6 = bf16[4,4,8192]{2,1,0:T(4,128)(2,1)S(1)} slice(bf16[8,4,8192]{2,1,0:T(4,128)(2,1)} %param.12), slice={[0:4], [0:4], [0:8192]} | slice | bytes 524288 | tf_op jit(solution)/shard_map/slice | solution.py:307
  1.0 0.3 reshape.12.refs_0_
  1.3 4.6 %collective-permute-start = (bf16[16,64,128]{2,1,0:T(8,128)(2,1)S(1)}, bf16[16,64,128]{2,1,0:T(8,128)(2,1)S(1)}, u32[]{:S(2)}, u32[]{:S(2)}) collective-permute-start(bf16[16,64,128]{2,1,0:T(8,128)(2,1)S(1)} %reshape.12.refs_0_), channel_id=1, source_target_pairs={{0,1},{1,2},{2,3},{3,4},{4,5},{5,6},{6,7},{7,8},{8,9},{9,10},{10,1... | collective-permute-start | bytes 786440 | tf_op jit(solution)/shard_map/ppermute | solution.py:310
  5.9 1.0 %slice.7 = bf16[4,4,8192]{2,1,0:T(4,128)(2,1)S(1)} slice(bf16[8,4,8192]{2,1,0:T(4,128)(2,1)} %param.12), slice={[4:8], [0:4], [0:8192]} | slice | bytes 524288 | tf_op jit(solution)/shard_map/slice | solution.py:307
  7.0 0.3 reshape.13.refs_1_
  7.3 1.9 %collective-permute-start.1 = (bf16[16,64,128]{2,1,0:T(8,128)(2,1)S(1)}, bf16[16,64,128]{2,1,0:T(8,128)(2,1)S(1)}, u32[]{:S(2)}, u32[]{:S(2)}) collective-permute-start(bf16[16,64,128]{2,1,0:T(8,128)(2,1)S(1)} %reshape.13.refs_1_), channel_id=1, source_target_pairs={{0,1},{1,2},{2,3},{3,4},{4,5},{5,6},{6,7},{7,8},{8,9},{9,10},{10,1... | collective-permute-start | bytes 786440 | tf_op jit(solution)/shard_map/ppermute | solution.py:310
  9.2 0.8 %reshape.15.refs_3_.refs_2_ = s32[32,256]{1,0:T(8,128)S(1)} reshape(s32[8192]{0:T(1024)} %param.14) | data formatting | bytes 65536 | tf_op jit(solution)/shard_map/reshape | solution.py:312
  10.0 1.1 %copy.15 = f32[1,8,128,128]{3,2,1,0:T(8,128)S(1)} copy(f32[1,8,128,128]{3,1,2,0:T(8,128)} %bitcast.5) | data formatting | bytes 1048576
  11.1 0.0 copy-start.8
  11.1 0.9 %copy-done.8 = bf16[256,256]{1,0:T(8,128)(2,1)S(1)} copy-done((bf16[256,256]{1,0:T(8,128)(2,1)S(1)}, bf16[256,256]{1,0:T(8,128)(2,1)}, u32[]{:S(2)}) %copy-start.8) | copy-done | bytes 131096
  12.0 0.0 copy-start
  12.0 0.0 copy-start.1
  12.0 0.0 copy-start.2
  12.0 0.0 copy-start.3
  12.0 0.0 copy-start.4
  12.0 0.0 copy-start.5
  12.1 0.0 copy-start.6
  12.1 0.0 copy-start.7
  12.1 2.6 %prep.1 = (f32[8,128,256]{2,1,0:T(8,128)S(1)}, f32[8,256,256]{2,1,0:T(8,128)S(1)}, bf16[256,8192]{1,0:T(8,128)(2,1)S(1)}) custom-call(bf16[16,64,128]{2,1,0:T(8,128)(2,1)S(1)} %reshape.12.refs_0_, bf16[16,64,128]{2,1,0:T(8,128)(2,1)S(1)} %reshape.13.refs_1_, f32[8,128,128]{2,1,0:T(8,128)S(1)} %bitcast.4, s32[32,256]{1,0:T(8,128)S(1)} %reshape.15.refs_3_.refs_2_, ...), custom_call_target="tpu_custom_call" | custom-call | flops 4000000000 | bytes 9437184 | tf_op jit(solution)/shard_map/prep/pallas_call | solution.py:315
  14.7 0.0 collective-permute-done.prev
  14.7 0.0 copy-done
  14.8 0.0 copy-done.1
  14.8 0.0 copy-done.2
  14.8 0.0 copy-done.3
  14.8 0.0 copy-done.4
  14.8 0.0 copy-done.5
  14.8 0.0 copy-done.6
  14.8 0.0 copy-done.7
  14.8 3.3 %filter.1.refs_0_ = f32[1024,128]{1,0:T(8,128)S(1)} custom-call(bf16[16,64,128]{2,1,0:T(8,128)(2,1)S(1)} %collective-permute-done.prev, f32[8,128,256]{2,1,0:T(8,128)S(1)} %get-tuple-element.13.gain.refs_4_, f32[8,256,256]{2,1,0:T(8,128)S(1)} %get-tuple-element.14.part.refs_5_, bf16[256,256]{1,0:T(8,128)(2,1)S(1)} %copy-done, ...), custom_call_target="tpu_custom_call" | custom-call | flops 4000000000 | bytes 4194304 | tf_op jit(solution)/shard_map/filter/pallas_call | solution.py:334
  18.1 0.0 collective-permute-done.1.refs_3_
  18.1 24.8 %work.1 = f32[8,4,32]{2,1,0:T(4,128)S(1)} custom-call(f32[1024,128]{1,0:T(8,128)S(1)} %filter.1.refs_0_, bf16[256,8192]{1,0:T(8,128)(2,1)S(1)} %get-tuple-element.15.refs_1_, s32[32,256]{1,0:T(8,128)S(1)} %reshape.15.refs_3_.refs_2_, bf16[16,64,128]{2,1,0:T(8,128)(2,1)S(1)} %collective-permute-done.1.refs_3_, ...), custom_call_target="tpu_custom_call" | custom-call | tf_op jit(solution)/shard_map/work/pallas_call | solution.py:347
  43.0 0.6 %copy.17 = f32[8,4,32]{2,1,0:T(4,128)} copy(f32[8,4,32]{2,1,0:T(4,128)S(1)} %work.1) | data formatting | bytes 8192
Async XLA Ops:
  1.3 13.4 %collective-permute-start = (bf16[16,64,128]{2,1,0:T(8,128)(2,1)S(1)}, bf16[16,64,128]{2,1,0:T(8,128)(2,1)S(1)}, u32[]{:S(2)}, u32[]{:S(2)}) collective-permute-start(bf16[16,64,128]{2,1,0:T(8,128)(2,1)S(1)} %reshape.12.refs_0_), channel_id=1, source_target_pairs={{0,1},{1,2},{2,3},{3,4},{4,5},{5,6},{6,7},{7,8},{8,9},{9,10},{10,1... | collective-permute-start | bytes 786440 | tf_op jit(solution)/shard_map/ppermute | solution.py:310
  7.3 10.8 %collective-permute-start.1 = (bf16[16,64,128]{2,1,0:T(8,128)(2,1)S(1)}, bf16[16,64,128]{2,1,0:T(8,128)(2,1)S(1)}, u32[]{:S(2)}, u32[]{:S(2)}) collective-permute-start(bf16[16,64,128]{2,1,0:T(8,128)(2,1)S(1)} %reshape.13.refs_1_), channel_id=1, source_target_pairs={{0,1},{1,2},{2,3},{3,4},{4,5},{5,6},{6,7},{7,8},{8,9},{9,10},{10,1... | collective-permute-start | bytes 786440 | tf_op jit(solution)/shard_map/ppermute | solution.py:310
  11.1 0.9 %copy-start.8 = (bf16[256,256]{1,0:T(8,128)(2,1)S(1)}, bf16[256,256]{1,0:T(8,128)(2,1)}, u32[]{:S(2)}) copy-start(bf16[256,256]{1,0:T(8,128)(2,1)} %constant.18.clone.refs_4_) | copy-start | bytes 393220
  12.0 2.7 %copy-start = (bf16[256,256]{1,0:T(8,128)(2,1)S(1)}, bf16[256,256]{1,0:T(8,128)(2,1)}, u32[]{:S(2)}) copy-start(bf16[256,256]{1,0:T(8,128)(2,1)} %constant.19.clone.left.refs_6_) | copy-start | bytes 393220
  12.0 2.7 %copy-start.1 = (bf16[256,256]{1,0:T(8,128)(2,1)S(1)}, bf16[256,256]{1,0:T(8,128)(2,1)}, u32[]{:S(2)}) copy-start(bf16[256,256]{1,0:T(8,128)(2,1)} %constant.20.clone.right_h.refs_7_) | copy-start | bytes 393220
  12.0 2.7 %copy-start.2 = (bf16[256,256]{1,0:T(8,128)(2,1)S(1)}, bf16[256,256]{1,0:T(8,128)(2,1)}, u32[]{:S(2)}) copy-start(bf16[256,256]{1,0:T(8,128)(2,1)} %constant.21.clone.right_l.refs_8_) | copy-start | bytes 393220
  12.0 2.7 %copy-start.3 = (bf16[256,256]{1,0:T(8,128)(2,1)S(1)}, bf16[256,256]{1,0:T(8,128)(2,1)}, u32[]{:S(2)}) copy-start(bf16[256,256]{1,0:T(8,128)(2,1)} %constant.22.clone.back_right_h.refs_9_) | copy-start | bytes 393220
  12.0 2.8 %copy-start.4 = (bf16[256,256]{1,0:T(8,128)(2,1)S(1)}, bf16[256,256]{1,0:T(8,128)(2,1)}, u32[]{:S(2)}) copy-start(bf16[256,256]{1,0:T(8,128)(2,1)} %constant.23.clone.back_right_l.refs_10_) | copy-start | bytes 393220
  12.0 2.8 %copy-start.5 = (f32[128,256]{1,0:T(8,128)S(1)}, f32[128,256]{1,0:T(8,128)}, u32[]{:S(2)}) copy-start(f32[128,256]{1,0:T(8,128)} %constant.26.clone.twist.refs_13_) | copy-start | bytes 393220
  12.1 2.7 %copy-start.6 = (bf16[128,256]{1,0:T(8,128)(2,1)S(1)}, bf16[128,256]{1,0:T(8,128)(2,1)}, u32[]{:S(2)}) copy-start(bf16[128,256]{1,0:T(8,128)(2,1)} %constant.24.clone.back_left_h.refs_11_) | copy-start | bytes 196612
  12.1 2.7 %copy-start.7 = (bf16[128,256]{1,0:T(8,128)(2,1)S(1)}, bf16[128,256]{1,0:T(8,128)(2,1)}, u32[]{:S(2)}) copy-start(bf16[128,256]{1,0:T(8,128)(2,1)} %constant.25.clone.back_left_l.refs_12_) | copy-start | bytes 196612
